TPU v7x, 256 devices: a whole 4x4x8 slice. The times are simulated.
256 devices in a mesh: trow: 32 (over z, x), tcol: 8 (over y, core).
Axes of the slice: x: 4, y: 4, z: 8, core: 2. Of those that a mesh axis runs over, the one named last changes fastest.
Arguments:
- query: bfloat16 [64, 512, 1152], P('trow', 'tcol'), may hold values from -64 to 64
- key: bfloat16 [64, 512, 1152], P('trow', 'tcol'), may hold values from -6 to 6
- value: bfloat16 [64, 512, 1152], P('trow', 'tcol'), may hold values from -6 to 6
- control: bfloat16 [64, 512, 1152], P('trow', 'tcol'), may hold values from -6 to 6
- kernel: float32 [3, 3, 1152], replicated, may hold values from -3 to 3
- grad_out: bfloat16 [64, 512, 1152], P('trow', 'tcol'), may hold values from -96 to 96
- detail_blocks: int32 [32, 8, 8], P('trow'), may hold values from -1 to 0, as said below
Outputs:
- grad_query: bfloat16 [64, 512, 1152], P('trow', 'tcol')
- grad_key: bfloat16 [64, 512, 1152], P('trow', 'tcol')
- grad_value: bfloat16 [64, 512, 1152], P('trow', 'tcol')
- grad_control: bfloat16 [64, 512, 1152], P('trow', 'tcol')
- grad_kernel: float32 [3, 3, 1152], replicated
Inputs may be any that keep to these rules, and one draw needn't show every extreme that they name: `detail_blocks`: entry [i, j, p] is the key block of tile (i, p) that tile (i, j) also attends to, or -1 for none; entry [i, j, j] is -1; each tile names blocks of 1 to 7 other tiles, and in every tile row one tile names a block of each of the other 7 tiles.
All inputs are finite; a program needn't handle non-finite values.
Results may differ from a plain program's by a relative error of at most 0.0095.
Values may be sent and summed in bfloat16 or wider, within the bound.
A program may use at most 128 MiB of HBM per device.

v0:
```python
import math

import jax
import jax.numpy as jnp
from jax import lax
from jax.sharding import PartitionSpec as P

HEADS = 16
HEAD_DIM = 72
BLOCK = 128


NEG = -1e30


def with_halo(block, sides, width):
    for axis, dim in sides:
        count = lax.axis_size(axis)
        forward = [(i, i + 1) for i in range(count - 1)]
        backward = [(target, source) for source, target in forward]
        low = lax.ppermute(
            lax.slice_in_dim(block, block.shape[dim] - width, None, axis=dim), axis, forward
        )
        high = lax.ppermute(lax.slice_in_dim(block, 0, width, axis=dim), axis, backward)
        block = jnp.concatenate([low, block, high], axis=dim)
    return block


def from_behind(shard, axis, by):
    length = lax.axis_size(axis)
    pairs = [(i, i + by) for i in range(length) if 0 <= i + by < length]
    return lax.ppermute(shard, axis, pairs)


def conv_taps(padded, kernel, rows, cols):
    total = jnp.zeros((rows, cols, padded.shape[2]), jnp.float32)
    for row_off in range(3):
        for col_off in range(3):
            total = (
                total
                + kernel[row_off, col_off][None, None, :]
                * padded[row_off : row_off + rows, col_off : col_off + cols]
            )
    return total


def conv_back(padded, kernel, rows, cols):
    total = jnp.zeros((rows, cols, padded.shape[2]), jnp.float32)
    for row_off in range(3):
        for col_off in range(3):
            total = (
                total
                + kernel[row_off, col_off][None, None, :]
                * padded[2 - row_off : 2 - row_off + rows, 2 - col_off : 2 - col_off + cols]
            )
    return total


def attend_group(queries, grads, keys, values, key_live):
    inv_root = HEAD_DIM ** (-0.5)
    scores = (
        jnp.einsum("qhd,khd->hqk", queries, keys, preferred_element_type=jnp.float32) * inv_root
    )
    scores = jnp.where(key_live[None, None, :], scores, NEG)
    row_top = jnp.max(scores, axis=2, keepdims=True)
    raised = jnp.exp(scores - row_top)
    weights = raised / jnp.sum(raised, axis=2, keepdims=True)
    weights_bf = weights.astype(jnp.bfloat16)
    attn_out = jnp.einsum("hqk,khd->qhd", weights_bf, values, preferred_element_type=jnp.float32)
    row_delta = jnp.sum(grads.astype(jnp.float32) * attn_out, axis=2)
    grad_weights = jnp.einsum("qhd,khd->hqk", grads, values, preferred_element_type=jnp.float32)
    grad_scores = weights * (grad_weights - jnp.transpose(row_delta)[:, :, None])
    grad_scores_bf = grad_scores.astype(jnp.bfloat16)
    grad_q = (
        jnp.einsum("hqk,khd->qhd", grad_scores_bf, keys, preferred_element_type=jnp.float32)
        * inv_root
    )
    grad_k = (
        jnp.einsum("hqk,qhd->khd", grad_scores_bf, queries, preferred_element_type=jnp.float32)
        * inv_root
    )
    grad_v = jnp.einsum("hqk,qhd->khd", weights_bf, grads, preferred_element_type=jnp.float32)
    return (grad_q, grad_k, grad_v)


def per_device(query, key, value, control, kernel, grad_out, detail_blocks):
    tile_rows, tile_column_count, channels = query.shape
    tile_tokens = tile_rows * tile_column_count
    tile_blocks = tile_tokens // BLOCK
    row_count = lax.axis_size("trow")
    col_count = lax.axis_size("tcol")
    my_row = lax.axis_index("trow")
    my_col = lax.axis_index("tcol")
    control_ext = with_halo(control, (("trow", 0), ("tcol", 1)), 1).astype(jnp.float32)
    v_ctrl = (
        value.astype(jnp.float32) + conv_taps(control_ext, kernel, tile_rows, tile_column_count)
    ).astype(jnp.bfloat16)
    query_flat = query.reshape(tile_tokens, channels)
    key_flat = key.reshape(tile_tokens, channels)
    value_flat = v_ctrl.reshape(tile_tokens, channels)
    grad_flat = grad_out.reshape(tile_tokens, channels)
    above = from_behind((key_flat, value_flat), "trow", 1)
    below = from_behind((key_flat, value_flat), "trow", -1)
    pattern = detail_blocks[0]
    wanted = lax.dynamic_index_in_dim(pattern, my_col, 0, keepdims=False)
    asked = lax.dynamic_index_in_dim(pattern, my_col, 1, keepdims=False)
    slot_ids = jnp.arange(col_count - 1, dtype=jnp.int32)
    others = slot_ids + (slot_ids >= my_col).astype(jnp.int32)
    wanted_others = wanted[others]
    row_keys, row_values = (
        lax.all_gather(key_flat, "tcol", axis=0, tiled=True),
        lax.all_gather(value_flat, "tcol", axis=0, tiled=True),
    )
    picked = others * tile_blocks + jnp.maximum(wanted_others, 0)
    detail_keys = row_keys.reshape(col_count * tile_blocks, BLOCK, channels)[picked]
    detail_values = row_values.reshape(col_count * tile_blocks, BLOCK, channels)[picked]
    detail_count = (col_count - 1) * BLOCK
    all_keys = jnp.concatenate(
        [key_flat, above[0], below[0], detail_keys.reshape(detail_count, channels)], axis=0
    )
    all_values = jnp.concatenate(
        [value_flat, above[1], below[1], detail_values.reshape(detail_count, channels)], axis=0
    )
    key_live = jnp.concatenate(
        [
            jnp.ones((tile_tokens,), bool),
            jnp.full((tile_tokens,), my_row >= 1),
            jnp.full((tile_tokens,), my_row + 1 < row_count),
            jnp.repeat(wanted_others >= 0, BLOCK),
        ],
        axis=0,
    )
    head_group = math.gcd(HEADS, 4)
    col_span = head_group * HEAD_DIM
    query_parts = []
    key_parts = []
    value_parts = []
    for group_index in range(HEADS // head_group):
        low = group_index * col_span
        high = low + col_span
        grad_q, grad_k, grad_v = attend_group(
            query_flat[:, low:high].reshape(-1, head_group, HEAD_DIM),
            grad_flat[:, low:high].reshape(-1, head_group, HEAD_DIM),
            all_keys[:, low:high].reshape(-1, head_group, HEAD_DIM),
            all_values[:, low:high].reshape(-1, head_group, HEAD_DIM),
            key_live,
        )
        query_parts.append(grad_q.reshape(-1, col_span))
        key_parts.append(grad_k.reshape(-1, col_span))
        value_parts.append(grad_v.reshape(-1, col_span))
    query_gradient_total = jnp.concatenate(query_parts, axis=1)
    grad_k_all = jnp.concatenate(key_parts, axis=1)
    grad_v_all = jnp.concatenate(value_parts, axis=1)
    up_terms = from_behind(
        (grad_k_all[tile_tokens : 2 * tile_tokens], grad_v_all[tile_tokens : 2 * tile_tokens]),
        "trow",
        -1,
    )
    down_terms = from_behind(
        (
            grad_k_all[2 * tile_tokens : 3 * tile_tokens],
            grad_v_all[2 * tile_tokens : 3 * tile_tokens],
        ),
        "trow",
        1,
    )
    slot_k = (
        grad_k_all[3 * tile_tokens :].reshape(col_count - 1, BLOCK, channels).astype(jnp.bfloat16)
    )
    slot_v = (
        grad_v_all[3 * tile_tokens :].reshape(col_count - 1, BLOCK, channels).astype(jnp.bfloat16)
    )
    detail_k = jnp.zeros((col_count, BLOCK, channels), jnp.bfloat16).at[others].set(slot_k)
    detail_v = jnp.zeros((col_count, BLOCK, channels), jnp.bfloat16).at[others].set(slot_v)
    returned_keys, returned_values = (
        lax.all_to_all(detail_k, "tcol", split_axis=0, concat_axis=0, tiled=True),
        lax.all_to_all(detail_v, "tcol", split_axis=0, concat_axis=0, tiled=True),
    )
    tile_owner_lookup = (
        asked[None, :] == jnp.arange(tile_blocks, dtype=jnp.int32)[:, None]
    ).astype(jnp.bfloat16)
    served_keys = jnp.einsum(
        "ev,vsw->esw", tile_owner_lookup, returned_keys, preferred_element_type=jnp.float32
    ).reshape(tile_tokens, channels)
    served_values = jnp.einsum(
        "ev,vsw->esw", tile_owner_lookup, returned_values, preferred_element_type=jnp.float32
    ).reshape(tile_tokens, channels)
    grad_key = (grad_k_all[:tile_tokens] + up_terms[0] + down_terms[0] + served_keys).astype(
        jnp.bfloat16
    )
    grad_value = (grad_v_all[:tile_tokens] + up_terms[1] + down_terms[1] + served_values).astype(
        jnp.bfloat16
    )
    grad_value_img = grad_value.reshape(tile_rows, tile_column_count, channels)
    value_ext = with_halo(grad_value_img, (("trow", 0), ("tcol", 1)), 1).astype(jnp.float32)
    grad_control = conv_back(value_ext, kernel, tile_rows, tile_column_count).astype(jnp.bfloat16)
    grad_value_f = grad_value_img.astype(jnp.float32)
    kernel_rows = []
    for row_off in range(3):
        kernel_cols = []
        for col_off in range(3):
            kernel_cols.append(
                jnp.sum(
                    control_ext[
                        row_off : row_off + tile_rows, col_off : col_off + tile_column_count
                    ]
                    * grad_value_f,
                    axis=(0, 1),
                )
            )
        kernel_rows.append(jnp.stack(kernel_cols, axis=0))
    grad_kernel = lax.psum(jnp.stack(kernel_rows, axis=0), ("trow", "tcol"))
    grad_query = query_gradient_total.astype(jnp.bfloat16).reshape(
        tile_rows, tile_column_count, channels
    )
    return (
        grad_query,
        grad_key.reshape(tile_rows, tile_column_count, channels),
        grad_value_img,
        grad_control,
        grad_kernel,
    )


def solution(mesh):
    return jax.shard_map(
        per_device,
        mesh=mesh,
        in_specs=(
            P("trow", "tcol", None),
            P("trow", "tcol", None),
            P("trow", "tcol", None),
            P("trow", "tcol", None),
            P(),
            P("trow", "tcol", None),
            P("trow", None, None),
        ),
        out_specs=(
            P("trow", "tcol", None),
            P("trow", "tcol", None),
            P("trow", "tcol", None),
            P("trow", "tcol", None),
            P(),
        ),
        check_vma=False,
    )
```

profile of v0, /device:TPU:1, one launch (start us, length us, event | category | flops | bytes accessed | tf_op | source)
XLA Modules:
  0.0 365.8 jit_solution(7707213717412692028)
XLA Ops:
  9.3 5.3 %collective-permute-start = (bf16[128,1152]{1,0:T(8,128)(2,1)}, bf16[128,1152]{1,0:T(8,128)(2,1)}, u32[]{:S(2)}, u32[]{:S(2)}) collective-permute-start(bf16[128,1152]{1,0:T(8,128)(2,1)} %bitcast.267), channel_id=1, source_target_pairs={{0,8},{8,16},{16,24},{24,32},{32,40},{40,48},{48,56},{56,64},{64,7... | collective-permute-start | bytes 884744 | tf_op jit(solution)/shard_map/ppermute | solution.py:32
  24.2 4.9 %collective-permute-start.5 = (bf16[4,1,1152]{2,1,0:T(2,128)(2,1)S(1)}, bf16[4,1,1152]{2,1,0:T(2,128)(2,1)S(1)}, u32[]{:S(2)}, u32[]{:S(2)}) collective-permute-start(bf16[4,1,1152]{2,1,0:T(2,128)(2,1)S(1)} %get-tuple-element.43), channel_id=1, source_target_pairs={{1,0},{2,1},{3,2},{4,3},{5,4},{6,5},{7,6},{9,8},{10,9},{11,10},{12... | collective-permute-start | bytes 27656 | tf_op jit(solution)/shard_map/ppermute | solution.py:24
  40.7 5.8 %collective-permute-start.6 = (bf16[128,1152]{1,0:T(8,128)(2,1)}, bf16[128,1152]{1,0:T(8,128)(2,1)}, u32[]{:S(2)}, u32[]{:S(2)}) collective-permute-start(bf16[128,1152]{1,0:T(8,128)(2,1)} %bitcast.12), channel_id=1, source_target_pairs={{0,8},{8,16},{16,24},{24,32},{32,40},{40,48},{48,56},{56,64},{64,7... | collective-permute-start | bytes 884744 | tf_op jit(solution)/shard_map/ppermute | solution.py:32
  55.6 4.0 %fusion.108 = (f32[4,128]{1,0:T(4,128)S(1)}, f32[4,128,1280]{1,2,0:T(8,128)}) fusion(bf16[1280,4,72]{0,2,1:T(8,128)(2,1)} %bitcast.257, bf16[128,4,72]{0,2,1:T(8,128)(2,1)S(1)} %bitcast.287, pred[1280]{0:T(1024)(128)(4,1)S(1)} %copy-done.47), kind=kOutput, calls=%fused_computation.197 | convolution fusion | flops 96994560 | bytes 3435776 | tf_op jit(solution)/shard_map/sub | solution.py:66
  80.9 3.6 fusion.107
  92.5 3.5 fusion.106
  103.9 8.9 %concatenate.51 = f32[1280,1152]{1,0:T(8,128)} concatenate(f32[1280,288]{1,0:T(8,128)} %copy.87, f32[1280,288]{1,0:T(8,128)} %copy.88, f32[1280,288]{1,0:T(8,128)} %copy.89, f32[1280,288]{1,0:T(8,128)} %copy.90), dimensions={1} | concatenate | bytes 11796480 | tf_op jit(solution)/shard_map/concatenate | solution.py:153
  112.8 3.7 %slice.404 = bf16[896,1152]{1,0:T(8,128)(2,1)} slice(f32[1280,1152]{1,0:T(8,128)} %concatenate.51), slice={[384:1280], [0:1152]} | slice | bytes 4128768 | tf_op jit(solution)/shard_map/slice | solution.py:171
  118.9 3.7 %collective-permute-start.11 = (f32[128,1152]{1,0:T(8,128)}, f32[128,1152]{1,0:T(8,128)}, u32[]{:S(2)}, u32[]{:S(2)}) collective-permute-start(f32[128,1152]{1,0:T(8,128)} %get-tuple-element.29), channel_id=1, source_target_pairs={{0,8},{8,16},{16,24},{24,32},{32,40},{40,48},{48,56},{56,64},{64,7... | collective-permute-start | bytes 1769480 | tf_op jit(solution)/shard_map/ppermute | solution.py:32
  125.6 5.8 %scatter_fusion.1 = bf16[8,128,1152]{2,1,0:T(8,128)(2,1)} fusion(bf16[8,128,1152]{2,1,0:T(8,128)(2,1)} %broadcast.125.clone.1, s32[7]{0:T(128)S(1)} %copy-done.44, bf16[7,128,1152]{2,1,0:T(8,128)(2,1)} %bitcast.233), kind=kCustom, calls=%fused_computation.4 | custom fusion | bytes 6193180 | tf_op jit(solution)/shard_map/scatter | solution.py:174
  131.4 4.7 %all-to-all-start.1 = ((bf16[8,128,1152]{2,1,0:T(8,128)(2,1)}), bf16[8,128,1152]{2,1,0:T(8,128)(2,1)}, u32[]{:S(2)}, u32[]{:S(2)}) async-start(bf16[8,128,1152]{2,1,0:T(8,128)(2,1)} %scatter_fusion.1), calls=%async_computation.1 | async-start | bytes 4718592 | tf_op jit(solution)/shard_map/all_to_all | solution.py:177
  136.2 3.9 %gather_fusion.2 = bf16[7,128,1152]{2,1,0:T(8,128)(2,1)} fusion(bf16[8,128,1152]{2,1,0:T(8,128)(2,1)} %bitcast.264, s32[1024]{0:T(1024)} %pad_clamp_fusion), kind=kCustom, calls=%fused_computation.2 | custom fusion | bytes 4128796 | tf_op jit(solution)/shard_map/gather | solution.py:116
  142.1 3.6 fusion.100
  176.4 6.4 %pad_maximum_fusion.2 = bf16[2,64,1152]{1,0,2:T(2,128)(2,1)S(1)} fusion(bf16[2,64,288]{1,0,2:T(2,128)(2,1)S(1)} %concatenate.48, bf16[2,64,288]{1,0,2:T(2,128)(2,1)S(1)} %concatenate.47, bf16[2,64,288]{1,0,2:T(2,128)(2,1)} %concatenate.46, bf16[2,64,288]{1,0,2:T(2,128)(2,1)} %concatenate.45), kind=kLoop, calls=%fused_computation.135 | loop fusion | flops 442368 | bytes 589824 | tf_op jit(solution)/shard_map/concatenate | solution.py:151
  189.1 3.4 convolution_multiply_fusion.6
  195.2 3.3 convolution_multiply_fusion.5
  201.4 3.4 convolution_multiply_fusion.4
  207.5 8.5 %concatenate.50 = f32[1280,1152]{1,0:T(8,128)} concatenate(f32[1280,288]{1,0:T(8,128)S(1)} %copy.79, f32[1280,288]{1,0:T(8,128)} %copy.80, f32[1280,288]{1,0:T(8,128)} %copy.81, f32[1280,288]{1,0:T(8,128)} %copy.82), dimensions={1} | concatenate | bytes 11796480 | tf_op jit(solution)/shard_map/concatenate | solution.py:152
  220.8 5.1 %collective-permute-start.9 = (f32[128,1152]{1,0:T(8,128)}, f32[128,1152]{1,0:T(8,128)}, u32[]{:S(2)}, u32[]{:S(2)}) collective-permute-start(f32[128,1152]{1,0:T(8,128)} %get-tuple-element.31), channel_id=1, source_target_pairs={{0,8},{8,16},{16,24},{24,32},{32,40},{40,48},{48,56},{56,64},{64,7... | collective-permute-start | bytes 1769480 | tf_op jit(solution)/shard_map/ppermute | solution.py:32
  228.9 5.1 %scatter_fusion = bf16[8,128,1152]{2,1,0:T(8,128)(2,1)} fusion(bf16[8,128,1152]{2,1,0:T(8,128)(2,1)} %broadcast.125.clone, s32[7]{0:T(128)S(1)} %copy-done.45, bf16[7,128,1152]{2,1,0:T(8,128)(2,1)S(1)} %bitcast.232), kind=kCustom, calls=%fused_computation.3 | custom fusion | bytes 6193180 | tf_op jit(solution)/shard_map/scatter | solution.py:173
  234.0 5.2 %all-to-all-start = ((bf16[8,128,1152]{2,1,0:T(8,128)(2,1)}), bf16[8,128,1152]{2,1,0:T(8,128)(2,1)}, u32[]{:S(2)}, u32[]{:S(2)}) async-start(bf16[8,128,1152]{2,1,0:T(8,128)(2,1)} %scatter_fusion), calls=%async_computation | async-start | bytes 4718592 | tf_op jit(solution)/shard_map/all_to_all | solution.py:176
  245.4 5.6 %collective-permute-start.12 = (bf16[1,64,1152]{2,1,0:T(8,128)(2,1)S(1)}, bf16[1,64,1152]{2,1,0:T(8,128)(2,1)S(1)}, u32[]{:S(2)}, u32[]{:S(2)}) collective-permute-start(bf16[1,64,1152]{2,1,0:T(8,128)(2,1)S(1)} %get-tuple-element.44), channel_id=1, source_target_pairs={{0,8},{8,16},{16,24},{24,32},{32,40},{40,48},{48,56},{56,64},{64,7... | collective-permute-start | bytes 442376 | tf_op jit(solution)/shard_map/ppermute | solution.py:21
  251.8 94.0 %psum.7 = f32[3,3,1152]{2,1,0:T(4,128)} all-reduce(f32[3,3,1152]{2,1,0:T(4,128)S(1)} %pad_maximum_fusion.3), channel_id=1, replica_groups=mesh['trow'=32,'tcol'=8] {'trow','tcol'}, use_global_device_ids=true, to_apply=%region_23.24 | all-reduce | flops 10368 | bytes 82944 | tf_op jit(solution)/shard_map/psum | solution.py:212
  351.4 3.3 fusion.34
  (233 shorter events, 145.5 us)
Async XLA Ops:
  7.2 39.3 %all-gather.3.cloned.1.call-start = ((), (), s32[]{:S(2)}) async-start(), calls=%async_computation.2 | async-start | bytes 2654208 | tf_op jit(solution)/shard_map/all_gather | solution.py:111
  7.9 128.2 %all-gather.5.cloned.1.call-start = ((), (), s32[]{:S(2)}) async-start(), calls=%async_computation.3 | async-start | bytes 2654208 | tf_op jit(solution)/shard_map/all_gather | solution.py:112
  8.0 41.2 %collective-permute-start.1 = (bf16[128,1152]{1,0:T(8,128)(2,1)}, bf16[128,1152]{1,0:T(8,128)(2,1)}, u32[]{:S(2)}, u32[]{:S(2)}) collective-permute-start(bf16[128,1152]{1,0:T(8,128)(2,1)} %bitcast.266), channel_id=1, source_target_pairs={{8,0},{16,8},{24,16},{32,24},{40,32},{48,40},{56,48},{64,56},{72,6... | collective-permute-start | bytes 884744 | tf_op jit(solution)/shard_map/ppermute | solution.py:32
  9.3 39.9 %collective-permute-start = (bf16[128,1152]{1,0:T(8,128)(2,1)}, bf16[128,1152]{1,0:T(8,128)(2,1)}, u32[]{:S(2)}, u32[]{:S(2)}) collective-permute-start(bf16[128,1152]{1,0:T(8,128)(2,1)} %bitcast.267), channel_id=1, source_target_pairs={{0,8},{8,16},{16,24},{24,32},{32,40},{40,48},{48,56},{56,64},{64,7... | collective-permute-start | bytes 884744 | tf_op jit(solution)/shard_map/ppermute | solution.py:32
  15.6 7.6 %collective-permute-start.2 = (bf16[1,64,1152]{2,1,0:T(8,128)(2,1)S(1)}, bf16[1,64,1152]{2,1,0:T(8,128)(2,1)S(1)}, u32[]{:S(2)}, u32[]{:S(2)}) collective-permute-start(bf16[1,64,1152]{2,1,0:T(8,128)(2,1)S(1)} %get-tuple-element.55), channel_id=1, source_target_pairs={{0,8},{8,16},{16,24},{24,32},{32,40},{40,48},{48,56},{56,64},{64,7... | collective-permute-start | bytes 442376 | tf_op jit(solution)/shard_map/ppermute | solution.py:21
  18.2 5.9 %collective-permute-start.3 = (bf16[1,64,1152]{2,1,0:T(8,128)(2,1)S(1)}, bf16[1,64,1152]{2,1,0:T(8,128)(2,1)S(1)}, u32[]{:S(2)}, u32[]{:S(2)}) collective-permute-start(bf16[1,64,1152]{2,1,0:T(8,128)(2,1)S(1)} %get-tuple-element.54), channel_id=1, source_target_pairs={{8,0},{16,8},{24,16},{32,24},{40,32},{48,40},{56,48},{64,56},{72,6... | collective-permute-start | bytes 442376 | tf_op jit(solution)/shard_map/ppermute | solution.py:24
  20.3 17.0 %copy-start.46 = (s32[1,8,8]{2,1,0:T(8,128)S(1)}, s32[1,8,8]{2,1,0:T(8,128)}, u32[]{:S(2)}) copy-start(s32[1,8,8]{2,1,0:T(8,128)} %param.13) | copy-start | bytes 772
  23.1 16.2 %copy-start.27 = (f32[1152]{0:T(1024)}, f32[1152]{0:T(1024)S(1)}, u32[]{:S(2)}) copy-start(f32[1152]{0:T(1024)S(1)} %get-tuple-element.21) | copy-start | bytes 13828
  23.1 16.2 %copy-start.29 = (f32[1152]{0:T(1024)}, f32[1152]{0:T(1024)S(1)}, u32[]{:S(2)}) copy-start(f32[1152]{0:T(1024)S(1)} %get-tuple-element.22) | copy-start | bytes 13828
  24.2 13.7 %collective-permute-start.5 = (bf16[4,1,1152]{2,1,0:T(2,128)(2,1)S(1)}, bf16[4,1,1152]{2,1,0:T(2,128)(2,1)S(1)}, u32[]{:S(2)}, u32[]{:S(2)}) collective-permute-start(bf16[4,1,1152]{2,1,0:T(2,128)(2,1)S(1)} %get-tuple-element.43), channel_id=1, source_target_pairs={{1,0},{2,1},{3,2},{4,3},{5,4},{6,5},{7,6},{9,8},{10,9},{11,10},{12... | collective-permute-start | bytes 27656 | tf_op jit(solution)/shard_map/ppermute | solution.py:24
  29.1 8.8 %collective-permute-start.4 = (bf16[4,1,1152]{2,1,0:T(2,128)(2,1)S(1)}, bf16[4,1,1152]{2,1,0:T(2,128)(2,1)S(1)}, u32[]{:S(2)}, u32[]{:S(2)}) collective-permute-start(bf16[4,1,1152]{2,1,0:T(2,128)(2,1)S(1)} %get-tuple-element.42), channel_id=1, source_target_pairs={{0,1},{1,2},{2,3},{3,4},{4,5},{5,6},{6,7},{8,9},{9,10},{10,11},{11... | collective-permute-start | bytes 27656 | tf_op jit(solution)/shard_map/ppermute | solution.py:21
  39.4 100.7 %collective-permute-start.7 = (bf16[128,1152]{1,0:T(8,128)(2,1)}, bf16[128,1152]{1,0:T(8,128)(2,1)}, u32[]{:S(2)}, u32[]{:S(2)}) collective-permute-start(bf16[128,1152]{1,0:T(8,128)(2,1)} %bitcast.12), channel_id=1, source_target_pairs={{8,0},{16,8},{24,16},{32,24},{40,32},{48,40},{56,48},{64,56},{72,6... | collective-permute-start | bytes 884744 | tf_op jit(solution)/shard_map/ppermute | solution.py:32
  40.7 99.4 %collective-permute-start.6 = (bf16[128,1152]{1,0:T(8,128)(2,1)}, bf16[128,1152]{1,0:T(8,128)(2,1)}, u32[]{:S(2)}, u32[]{:S(2)}) collective-permute-start(bf16[128,1152]{1,0:T(8,128)(2,1)} %bitcast.12), channel_id=1, source_target_pairs={{0,8},{8,16},{16,24},{24,32},{32,40},{40,48},{48,56},{56,64},{64,7... | collective-permute-start | bytes 884744 | tf_op jit(solution)/shard_map/ppermute | solution.py:32
  118.9 123.6 %collective-permute-start.11 = (f32[128,1152]{1,0:T(8,128)}, f32[128,1152]{1,0:T(8,128)}, u32[]{:S(2)}, u32[]{:S(2)}) collective-permute-start(f32[128,1152]{1,0:T(8,128)} %get-tuple-element.29), channel_id=1, source_target_pairs={{0,8},{8,16},{16,24},{24,32},{32,40},{40,48},{48,56},{56,64},{64,7... | collective-permute-start | bytes 1769480 | tf_op jit(solution)/shard_map/ppermute | solution.py:32
  122.6 119.9 %collective-permute-start.10 = (f32[128,1152]{1,0:T(8,128)}, f32[128,1152]{1,0:T(8,128)}, u32[]{:S(2)}, u32[]{:S(2)}) collective-permute-start(f32[128,1152]{1,0:T(8,128)} %get-tuple-element.28), channel_id=1, source_target_pairs={{8,0},{16,8},{24,16},{32,24},{40,32},{48,40},{56,48},{64,56},{72,6... | collective-permute-start | bytes 1769480 | tf_op jit(solution)/shard_map/ppermute | solution.py:32
  131.4 102.6 %all-to-all-start.1 = ((bf16[8,128,1152]{2,1,0:T(8,128)(2,1)}), bf16[8,128,1152]{2,1,0:T(8,128)(2,1)}, u32[]{:S(2)}, u32[]{:S(2)}) async-start(bf16[8,128,1152]{2,1,0:T(8,128)(2,1)} %scatter_fusion.1), calls=%async_computation.1 | async-start | bytes 4718592 | tf_op jit(solution)/shard_map/all_to_all | solution.py:177
  220.8 134.0 %collective-permute-start.9 = (f32[128,1152]{1,0:T(8,128)}, f32[128,1152]{1,0:T(8,128)}, u32[]{:S(2)}, u32[]{:S(2)}) collective-permute-start(f32[128,1152]{1,0:T(8,128)} %get-tuple-element.31), channel_id=1, source_target_pairs={{0,8},{8,16},{16,24},{24,32},{32,40},{40,48},{48,56},{56,64},{64,7... | collective-permute-start | bytes 1769480 | tf_op jit(solution)/shard_map/ppermute | solution.py:32
  225.9 128.9 %collective-permute-start.8 = (f32[128,1152]{1,0:T(8,128)}, f32[128,1152]{1,0:T(8,128)}, u32[]{:S(2)}, u32[]{:S(2)}) collective-permute-start(f32[128,1152]{1,0:T(8,128)} %get-tuple-element.30), channel_id=1, source_target_pairs={{8,0},{16,8},{24,16},{32,24},{40,32},{48,40},{56,48},{64,56},{72,6... | collective-permute-start | bytes 1769480 | tf_op jit(solution)/shard_map/ppermute | solution.py:32
  234.0 117.4 %all-to-all-start = ((bf16[8,128,1152]{2,1,0:T(8,128)(2,1)}), bf16[8,128,1152]{2,1,0:T(8,128)(2,1)}, u32[]{:S(2)}, u32[]{:S(2)}) async-start(bf16[8,128,1152]{2,1,0:T(8,128)(2,1)} %scatter_fusion), calls=%async_computation | async-start | bytes 4718592 | tf_op jit(solution)/shard_map/all_to_all | solution.py:176
  244.0 113.0 %copy-start.3 = (bf16[128,1152]{1,0:T(8,128)(2,1)}, bf16[128,1152]{1,0:T(8,128)(2,1)S(1)}, u32[]{:S(2)}) copy-start(bf16[128,1152]{1,0:T(8,128)(2,1)S(1)} %fusion.76) | copy-start | bytes 884740
  244.1 101.7 %collective-permute-start.13 = (bf16[1,64,1152]{2,1,0:T(8,128)(2,1)S(1)}, bf16[1,64,1152]{2,1,0:T(8,128)(2,1)S(1)}, u32[]{:S(2)}, u32[]{:S(2)}) collective-permute-start(bf16[1,64,1152]{2,1,0:T(8,128)(2,1)S(1)} %get-tuple-element.45), channel_id=1, source_target_pairs={{8,0},{16,8},{24,16},{32,24},{40,32},{48,40},{56,48},{64,56},{72,6... | collective-permute-start | bytes 442376 | tf_op jit(solution)/shard_map/ppermute | solution.py:24
  245.4 100.4 %collective-permute-start.12 = (bf16[1,64,1152]{2,1,0:T(8,128)(2,1)S(1)}, bf16[1,64,1152]{2,1,0:T(8,128)(2,1)S(1)}, u32[]{:S(2)}, u32[]{:S(2)}) collective-permute-start(bf16[1,64,1152]{2,1,0:T(8,128)(2,1)S(1)} %get-tuple-element.44), channel_id=1, source_target_pairs={{0,8},{8,16},{16,24},{24,32},{32,40},{40,48},{48,56},{56,64},{64,7... | collective-permute-start | bytes 442376 | tf_op jit(solution)/shard_map/ppermute | solution.py:21
  345.8 11.2 %collective-permute-start.15 = (bf16[4,1,1152]{2,1,0:T(2,128)(2,1)S(1)}, bf16[4,1,1152]{2,1,0:T(2,128)(2,1)S(1)}, u32[]{:S(2)}, u32[]{:S(2)}) collective-permute-start(bf16[4,1,1152]{2,1,0:T(2,128)(2,1)S(1)} %get-tuple-element.41), channel_id=1, source_target_pairs={{1,0},{2,1},{3,2},{4,3},{5,4},{6,5},{7,6},{9,8},{10,9},{11,10},{12... | collective-permute-start | bytes 27656 | tf_op jit(solution)/shard_map/ppermute | solution.py:24
  348.4 8.6 %collective-permute-start.14 = (bf16[4,1,1152]{2,1,0:T(2,128)(2,1)S(1)}, bf16[4,1,1152]{2,1,0:T(2,128)(2,1)S(1)}, u32[]{:S(2)}, u32[]{:S(2)}) collective-permute-start(bf16[4,1,1152]{2,1,0:T(2,128)(2,1)S(1)} %get-tuple-element.40), channel_id=1, source_target_pairs={{0,1},{1,2},{2,3},{3,4},{4,5},{5,6},{6,7},{8,9},{9,10},{10,11},{11... | collective-permute-start | bytes 27656 | tf_op jit(solution)/shard_map/ppermute | solution.py:21
  (44 other events, 251.4 us)
Sparse Core Ops, SparseCore 0:
  9.8 32.3 all-gather.2
  46.6 34.6 all-gather.4
where the time goes:
time: 373 us; the launch traced here: 366 us
  local copies, waits for them, and re-layouts  108 us (29%)
  blocking collectives  94 us (25%)
  matrix products  60.8 us (16%)
  starting transfers between devices  59.1 us (16%)
  other arithmetic  26.9 us (7%)
  between operations  15.5 us (4%)
    psum x1, blocking collectives, per_device(): grad_kernel = lax.psum(jnp.stack(kernel_rows, axis=0), ('trow', 'tcol'))  94 us
    ppermute x8, starting transfers between devices, from_behind(): return lax.ppermute(shard, axis, pairs)  25 us
    ppermute x4, starting transfers between devices, with_halo(): lax.ppermute(lax.slice_in_dim(block, block.shape[dim] - width, None, axis...  14 us
    sub x4, matrix products, attend_group(): raised = jnp.exp(scores - row_top)  13.8 us
    unnamed x107, local copies, waits for them, and re-layouts  13.2 us
    dot_general x4, matrix products, attend_group(): jnp.einsum('hqk,qhd->khd', grad_scores_bf, queries, preferred_element_typ...  13 us
    reshape x4, local copies, waits for them, and re-layouts, per_device(): value_parts.append(grad_v.reshape(-1, col_span))  11.4 us
    reshape x4, local copies, waits for them, and re-layouts, per_device(): key_parts.append(grad_k.reshape(-1, col_span))  10.2 us
  transfers between devices with their start and end apart: 20, of which 1 were waited for; matrix products, arithmetic and copies ran while one was open for 51% of the time, Pallas kernels for 0%

commit v1 on v0

v1 whole, which is shorter than its diff:
```python
import functools
import math

import jax
import jax.numpy as jnp
from jax import lax
from jax.experimental import pallas as pl
from jax.experimental.pallas import tpu as pltpu
from jax.sharding import PartitionSpec as P

HEADS = 16
HEAD_DIM = 72
PAD_DIM = 80
D = 1152
TOK = 128
NX = 4
NY = 4
TR = 32
TC = 8
NZ = TR // NX
LANES = D // 128
ROOT = HEAD_DIM ** (-0.5)
EXP_SCALE = ROOT * math.log2(math.e)
BIG = 1e30
MESH = pl.DeviceIdType.MESH
F32 = jnp.float32
BF16 = jnp.bfloat16
DIRS = ((-1, -1), (-1, 0), (-1, 1), (0, -1), (0, 1), (1, -1), (1, 0), (1, 1))


class Place:
    def __init__(self):
        self.tr = lax.axis_index("trow")
        self.tc = lax.axis_index("tcol")
        self.z = self.tr // NX
        self.x = self.tr % NX
        self.y = self.tc // 2
        self.c = self.tc % 2
        self.u = 2 * self.z + self.c

    def chain(self, step):
        u = self.u + step
        return (NX * (u // 2) + self.x, 2 * self.y + u % 2)

    def has_chain(self, step):
        u = self.u + step
        return (u >= 0) & (u < 2 * NZ)

    def has_dir(self, dr, dc):
        r = self.tr + dr
        c = self.tc + dc
        return (r >= 0) & (r < TR) & (c >= 0) & (c < TC)


def signal(sem, dev):
    pl.semaphore_signal(sem, inc=1, device_id=dev, device_id_type=MESH)


def entry_barrier(me, with_z):
    bar = pltpu.get_barrier_semaphore()
    total = jnp.int32(NX * TC - 1)
    for step in range(1, NX * TC):
        rank = (me.x * TC + me.tc + step) % (NX * TC)
        signal(bar, (NX * me.z + rank // TC, rank % TC))
    for step in (-1, 1):
        ok = me.has_chain(step)
        total = total + ok.astype(jnp.int32)

        @pl.when(ok)
        def _():
            signal(bar, me.chain(step))

    for dr, dc in DIRS:
        ok = me.has_dir(dr, dc)
        total = total + ok.astype(jnp.int32)

        @pl.when(ok)
        def _():
            signal(bar, (me.tr + dr, me.tc + dc))

    if with_z:
        for step in range(1, NZ):
            zz = (me.z + step) % NZ
            signal(bar, (NX * zz + me.x, me.tc))
        total = total + (NZ - 1)
    pl.semaphore_wait(bar, total)


def remote(src, dst, ssem, rsem, dev):
    return pltpu.make_async_remote_copy(
        src_ref=src, dst_ref=dst, send_sem=ssem, recv_sem=rsem, device_id=dev, device_id_type=MESH
    )


def start_or_local(is_self, src, dst, ssem, rsem, dev):
    @pl.when(is_self)
    def _():
        pltpu.make_async_copy(src, dst, rsem).start()

    @pl.when(jnp.logical_not(is_self))
    def _():
        remote(src, dst, ssem, rsem, dev).start()


def wait_sent(is_self, src, dst, ssem, rsem, dev):
    @pl.when(jnp.logical_not(is_self))
    def _():
        remote(src, dst, ssem, rsem, dev).wait_send()


def wait_bytes(ref, sem):
    pltpu.make_async_copy(ref, ref, sem).wait()


def halo_views(img, rows, cols, diag, dr, dc):
    row = 0 if dr < 0 else 1
    col = 0 if dc < 0 else 48
    if dc == 0:
        return img.at[row], rows.at[1 if dr < 0 else 0]
    if dr == 0:
        return img.at[:, pl.ds(col, 16), :], cols.at[1 if dc < 0 else 0]
    slot = (2 if dr < 0 else 0) + (1 if dc < 0 else 0)
    return img.at[row, pl.ds(col, 16), :], diag.at[slot]


def halo_start(me, img, rows, cols, diag, ssem, rsem):
    for at, (dr, dc) in enumerate(DIRS):
        src, dst = halo_views(img, rows, cols, diag, dr, dc)

        @pl.when(me.has_dir(dr, dc))
        def _():
            remote(src, dst, ssem.at[at], rsem.at[at], (me.tr + dr, me.tc + dc)).start()


def halo_wait(me, img, rows, cols, diag, ssem, rsem):
    for at, (dr, dc) in enumerate(DIRS):
        src, dst = halo_views(img, rows, cols, diag, dr, dc)

        @pl.when(me.has_dir(dr, dc))
        def _():
            remote(src, dst, ssem.at[at], rsem.at[at], (me.tr + dr, me.tc + dc)).wait_send()

        @pl.when(me.has_dir(-dr, -dc))
        def _():
            remote(src, dst, ssem.at[at], rsem.at[at], (me.tr - dr, me.tc - dc)).wait_recv()


def fill_ext(me, ext, img, rows, cols, diag):
    ext[1:3, 8:72, :] = img[...].astype(F32)
    up = me.has_dir(-1, 0)
    down = me.has_dir(1, 0)
    left = me.has_dir(0, -1)
    right = me.has_dir(0, 1)

    def put(ok, place, value):
        ext[place] = jnp.where(ok, value.astype(F32), 0.0)

    put(up, (0, slice(8, 72)), rows[0])
    put(down, (3, slice(8, 72)), rows[1])
    for r in range(2):
        put(left, (1 + r, slice(0, 8)), cols[0, r].astype(F32)[8:16])
        put(right, (1 + r, slice(72, 80)), cols[1, r].astype(F32)[0:8])
    put(up & left, (0, slice(0, 8)), diag[0].astype(F32)[8:16])
    put(up & right, (0, slice(72, 80)), diag[1].astype(F32)[0:8])
    put(down & left, (3, slice(0, 8)), diag[2].astype(F32)[8:16])
    put(down & right, (3, slice(72, 80)), diag[3].astype(F32)[0:8])


def to_heads(x, flip, out):
    for b in range(LANES):
        flip[pl.ds(b * 128, 128), :] = x(b).T
    zero = jnp.zeros((PAD_DIM - HEAD_DIM, TOK), F32)
    for h in range(HEADS):
        out[h] = jnp.concatenate([flip[pl.ds(h * HEAD_DIM, HEAD_DIM), :], zero], axis=0).astype(BF16)


def scatter_kernel(
    q, k, v, g, c, w, db,
    oq, og, ok, ov, om, oext,
    sq, sg, sk, sv, sm, flip, hrow, hcol, hdiag,
    asend, arecv, msend, mrecv, bsend, brecv, hsend, hrecv,
):
    me = Place()
    for p in range(TC):
        live = (db[0, me.tc, p] >= 0) | (me.tc == p)
        sm[pl.ds(p, 1), :] = jnp.full((1, TOK), jnp.where(live, 0.0, BIG), F32)
    entry_barrier(me, False)
    halo_start(me, c, hrow, hcol, hdiag, hsend, hrecv)
    r = me.x % 2

    def dest(h):
        dev = (NX * me.z + h // NY, 2 * (h % NY) + me.x // 2)
        return dev, (dev[0] == me.tr) & (dev[1] == me.tc)

    def head_copies(act, n, src, dst):
        for h in range(HEADS):
            dev, is_self = dest(h)
            act(is_self, src.at[h], dst.at[r, me.tc], asend.at[n, h], arecv.at[n, r], dev)

    def mask_copies(act):
        for h in range(HEADS):
            dev, is_self = dest(h)
            act(is_self, sm, om.at[r, me.tc], msend.at[h], mrecv, dev)

    own_k = ok.at[pl.ds(1, 2)]
    own_v = ov.at[pl.ds(1, 2)]
    to_heads(lambda b: k[:, :, b * 128 : b * 128 + 128].reshape(TOK, 128).astype(F32), flip, sk)
    head_copies(start_or_local, 0, sk, own_k)
    mask_copies(start_or_local)
    to_heads(lambda b: q[:, :, b * 128 : b * 128 + 128].reshape(TOK, 128).astype(F32), flip, sq)
    head_copies(start_or_local, 1, sq, oq)
    halo_wait(me, c, hrow, hcol, hdiag, hsend, hrecv)
    fill_ext(me, oext, c, hrow, hcol, hdiag)

    def v_block(b):
        lanes = slice(b * 128, b * 128 + 128)
        total = v[:, :, lanes].astype(F32)
        for a in range(3):
            for s in range(3):
                total = total + w[a, s, lanes][None, None, :] * oext[a : a + 2, 7 + s : 71 + s, lanes]
        return total.astype(BF16).astype(F32).reshape(TOK, 128)

    to_heads(v_block, flip, sv)
    head_copies(start_or_local, 2, sv, own_v)
    to_heads(lambda b: g[:, :, b * 128 : b * 128 + 128].reshape(TOK, 128).astype(F32), flip, sg)
    head_copies(start_or_local, 3, sg, og)

    def chain_copy(at, arr, buf, step):
        src, dst = (buf.at[1], buf.at[3]) if step < 0 else (buf.at[2], buf.at[0])
        return remote(src, dst, bsend.at[arr, at], brecv.at[arr, at], me.chain(step))

    for n, arr, buf in ((0, 0, ok), (2, 1, ov)):
        for at, step in enumerate((-1, 1)):
            wait_bytes(buf.at[1 + at], arecv.at[n, at])

            @pl.when(me.has_chain(step))
            def _():
                chain_copy(at, arr, buf, step).start()

        @pl.when(jnp.logical_not(me.has_chain(-1)))
        def _():
            buf[0] = jnp.zeros(buf.shape[1:], BF16)

        @pl.when(jnp.logical_not(me.has_chain(1)))
        def _():
            buf[3] = jnp.zeros(buf.shape[1:], BF16)

    for n, buf in ((1, oq), (3, og)):
        for at in range(2):
            wait_bytes(buf.at[at], arecv.at[n, at])
    wait_bytes(om, mrecv)
    for n, src, dst in ((0, sk, own_k), (1, sq, oq), (2, sv, own_v), (3, sg, og)):
        head_copies(wait_sent, n, src, dst)
    mask_copies(wait_sent)
    for arr, buf in ((0, ok), (1, ov)):
        for at, step in enumerate((-1, 1)):

            @pl.when(me.has_chain(step))
            def _():
                chain_copy(at, arr, buf, step).wait_send()

            @pl.when(me.has_chain(-step))
            def _():
                chain_copy(at, arr, buf, step).wait_recv()


def dot(a, b, ca, cb):
    return lax.dot_general(a, b, (((ca,), (cb,)), ((), ())), preferred_element_type=F32)


def attend_kernel(q, g, k, v, m, odq, odk, odv, kt, vt, s_buf, t_buf):
    me = Place()
    odk[...] = jnp.zeros(odk.shape, F32)
    odv[...] = jnp.zeros(odv.shape, F32)

    def flip_one(i, _):
        a = i // TC
        j = i % TC
        kt[a, j] = k[a, j].astype(F32).T.astype(BF16)
        vt[a, j] = v[a, j].astype(F32).T.astype(BF16)
        return 0

    lax.fori_loop(0, 4 * TC, flip_one, 0)

    def visit(i, _):
        r = i // (TC // 2)
        j = 2 * (i % (TC // 2))
        qs = [q[r, j], q[r, j + 1]]
        gs = [g[r, j], g[r, j + 1]]
        q2 = jnp.concatenate(qs, axis=1)
        g2 = jnp.concatenate(gs, axis=1)
        bias = []
        for p in range(TC):
            bias.append(jnp.concatenate([m[r, j, pl.ds(p, 1), :], m[r, j + 1, pl.ds(p, 1), :]], axis=1))
        above_dead = (me.u == 0) & (r == 0)
        below_dead = (me.u == 2 * NZ - 1) & (r == 1)
        for dead in (above_dead, below_dead):
            bias.append(jnp.full((1, 2 * TOK), jnp.where(dead, BIG, 0.0), F32))
        top = jnp.full((8, 2 * TOK), -3.0e38, F32)
        for p in range(TC + 2):
            if p < TC:
                s = dot(kt[1 + r, p], q2, 1, 0)
            else:
                a = r + 2 * (p - TC)
                s = jnp.concatenate([dot(kt[a, j + t], qs[t], 1, 0) for t in range(2)], axis=1)
            s_buf[p] = s
            top = jnp.maximum(top, jnp.max(s.reshape(TOK // 8, 8, 2 * TOK), axis=0) - bias[p])
        top = jnp.max(top, axis=0, keepdims=True) * EXP_SCALE
        total = jnp.zeros((8, 2 * TOK), F32)
        delta = jnp.zeros((8, 2 * TOK), F32)
        for p in range(TC + 2):
            e = jnp.exp2(s_buf[p] * EXP_SCALE - (top + bias[p]))
            if p < TC:
                gw = dot(vt[1 + r, p], g2, 1, 0)
            else:
                a = r + 2 * (p - TC)
                gw = jnp.concatenate([dot(vt[a, j + t], gs[t], 1, 0) for t in range(2)], axis=1)
            te = e * gw
            s_buf[p] = e
            t_buf[p] = te
            total = total + jnp.sum(e.reshape(TOK // 8, 8, 2 * TOK), axis=0)
            delta = delta + jnp.sum(te.reshape(TOK // 8, 8, 2 * TOK), axis=0)
        inv = 1.0 / jnp.sum(total, axis=0, keepdims=True)
        delta = jnp.sum(delta, axis=0, keepdims=True) * inv
        qn = (q2.astype(F32) * (inv * ROOT)).astype(BF16)
        gn = (g2.astype(F32) * inv).astype(BF16)
        dq = jnp.zeros((PAD_DIM, 2 * TOK), F32)
        for p in range(TC + 2):
            e = s_buf[p]
            ds = (t_buf[p] - e * delta).astype(BF16)
            eb = e.astype(BF16)
            if p < TC:
                dq = dq + dot(k[1 + r, p], ds, 1, 0)
                odk[1 + r, p] += dot(qn, ds, 1, 1)
                odv[1 + r, p] += dot(gn, eb, 1, 1)
            else:
                a = r + 2 * (p - TC)
                parts = []
                for t in range(2):
                    half = slice(t * TOK, (t + 1) * TOK)
                    parts.append(dot(k[a, j + t], ds[:, half], 1, 0))
                    odk[a, j + t] += dot(qn[:, half], ds[:, half], 1, 1)
                    odv[a, j + t] += dot(gn[:, half], eb[:, half], 1, 1)
                dq = dq + jnp.concatenate(parts, axis=1)
        dq = (dq * (inv * ROOT)).astype(BF16)
        odq[r, j] = dq[:, :TOK]
        odq[r, j + 1] = dq[:, TOK:]
        return 0

    lax.fori_loop(0, TC, visit, 0)


def from_heads(land, flip, put):
    for h in range(HEADS):
        flip[pl.ds(h * HEAD_DIM, HEAD_DIM), :] = land[h].astype(F32)[:HEAD_DIM]
    for b in range(LANES):
        put(b, flip[pl.ds(b * 128, 128), :].T)


def gather_kernel(
    dq, dk, dv, cext, w,
    oq, ok, ov, oc, ow,
    edge, elan, sk, sv, lq, lk, lv, flip, ext, hrow, hcol, hdiag,
    pieces, red1, red2, red3, red4, part2, part3, part4,
    csend, crecv, asend, arecv, hsend, hrecv, psend, precv,
):
    me = Place()
    for arr, src in ((0, dk), (1, dv)):
        edge[arr, 0] = src[0].astype(BF16)
        edge[arr, 1] = src[3].astype(BF16)
    entry_barrier(me, True)

    def chain_copy(arr, at, step):
        return remote(edge.at[arr, at], elan.at[arr, 1 - at], csend.at[arr, at], crecv.at[arr, at], me.chain(step))

    order = (1, 0)
    for arr in order:
        for at, step in enumerate((-1, 1)):

            @pl.when(me.has_chain(step))
            def _():
                chain_copy(arr, at, step).start()

    head = me.x * NY + me.y

    def tile_copies(act, n, src, dst):
        for r in range(2):
            for j in range(TC):
                dev = (NX * me.z + 2 * me.c + r, j)
                is_self = (dev[0] == me.tr) & (me.tc == j)
                act(is_self, src.at[r, j], dst.at[head], asend.at[n, r * TC + j], arecv.at[n], dev)

    tile_copies(start_or_local, 0, dq, lq)
    for arr, n, acc, out, land in ((1, 2, dv, sv, lv), (0, 1, dk, sk, lk)):
        for at, step in enumerate((-1, 1)):
            @pl.when(me.has_chain(-step))
            def _():
                chain_copy(arr, at, step).wait_recv()

            row = 1 - at
            ok_here = me.has_chain(-step)
            extra = jnp.where(ok_here, elan[arr, row].astype(F32), 0.0)
            out[row] = (acc[1 + row] + extra).astype(BF16)
        tile_copies(start_or_local, n, out, land)

    def out_block(out):
        def put(b, x):
            out[:, :, b * 128 : b * 128 + 128] = x.reshape(2, 64, 128).astype(BF16)

        return put

    wait_bytes(lq, arecv.at[0])
    from_heads(lq, flip, out_block(oq))
    wait_bytes(lv, arecv.at[2])
    from_heads(lv, flip, out_block(ov))
    halo_start(me, ov, hrow, hcol, hdiag, hsend, hrecv)
    for b in range(LANES):
        lanes = slice(b * 128, b * 128 + 128)
        gv = ov[:, :, lanes].astype(F32)
        for a in range(3):
            for s in range(3):
                prod = gv * cext[a : a + 2, 7 + s : 71 + s, lanes]
                t = (a * 3 + s) * LANES + b
                pieces[t // 11, pl.ds(t % 11, 1), :] = jnp.sum(prod.reshape(TOK, 128), axis=0, keepdims=True)

    def exchange(stage, count, mine, src, land, dev):
        def run(act):
            for other in range(count):
                view = src.at[other] if stage == 0 else src
                act(mine == other, view, land.at[mine], psend.at[stage, other], precv.at[stage], dev(other))

        run(start_or_local)
        return run

    runs = []
    runs.append(exchange(0, TC, me.tc, pieces, red1, lambda o: (me.tr, o)))
    wait_bytes(lk, arecv.at[1])
    from_heads(lk, flip, out_block(ok))
    wait_bytes(red1, precv.at[0])
    part2[...] = jnp.sum(red1[...], axis=0)
    runs.append(exchange(1, NX, me.x, part2, red2, lambda o: (NX * me.z + o, me.tc)))
    halo_wait(me, ov, hrow, hcol, hdiag, hsend, hrecv)
    fill_ext(me, ext, ov, hrow, hcol, hdiag)
    wait_bytes(red2, precv.at[1])
    part3[...] = jnp.sum(red2[...], axis=0)
    runs.append(exchange(2, NZ, me.z, part3, red3, lambda o: (NX * o + me.x, me.tc)))
    for b in range(LANES):
        lanes = slice(b * 128, b * 128 + 128)
        total = jnp.zeros((2, 64, 128), F32)
        for a in range(3):
            for s in range(3):
                total = total + w[a, s, lanes][None, None, :] * ext[2 - a : 4 - a, 9 - s : 73 - s, lanes]
        oc[:, :, lanes] = total.astype(BF16)
    wait_bytes(red3, precv.at[2])
    part4[...] = jnp.sum(red3[...], axis=0)
    runs.append(exchange(3, TC, me.tc, part4, red4, lambda o: (me.tr, o)))
    tile_copies(wait_sent, 0, dq, lq)
    tile_copies(wait_sent, 1, sk, lk)
    tile_copies(wait_sent, 2, sv, lv)
    for arr in order:
        for at, step in enumerate((-1, 1)):

            @pl.when(me.has_chain(step))
            def _():
                chain_copy(arr, at, step).wait_send()

    wait_bytes(red4, precv.at[3])
    for t in range(9 * LANES):
        tap, b = t // LANES, t % LANES
        ow[tap // 3, pl.ds(tap % 3, 1), b * 128 : b * 128 + 128] = red4[t // 11, pl.ds(t % 11, 1), :]
    for run in runs:
        run(wait_sent)


def vmem_specs(n):
    return [pl.BlockSpec(memory_space=pltpu.VMEM)] * n


def per_device(query, key, value, control, kernel, grad_out, detail_blocks):
    sds = jax.ShapeDtypeStruct
    heads = lambda n: sds((n, TC, PAD_DIM, TOK), BF16)
    sem = pltpu.SemaphoreType.DMA
    vm = pltpu.VMEM
    qh, gh, kh, vh, mask, cext = pl.pallas_call(
        scatter_kernel,
        out_shape=(heads(2), heads(2), heads(4), heads(4), sds((2, TC, 8, TOK), F32), sds((4, 80, D), F32)),
        in_specs=vmem_specs(6) + [pl.BlockSpec(memory_space=pltpu.SMEM)],
        out_specs=tuple(vmem_specs(6)),
        scratch_shapes=[vm((HEADS, PAD_DIM, TOK), BF16)] * 4
        + [vm((8, TOK), F32), vm((D, TOK), F32)]
        + [vm((2, 64, D), BF16), vm((2, 2, 16, D), BF16), vm((4, 16, D), BF16)]
        + [sem((4, HEADS)), sem((4, 2)), sem((HEADS,)), sem, sem((2, 2)), sem((2, 2)), sem((8,)), sem((8,))],
        compiler_params=pltpu.CompilerParams(collective_id=0, has_side_effects=True),
        name="scatter",
    )(query, key, value, grad_out, control, kernel, detail_blocks)
    acc = sds((4, TC, PAD_DIM, TOK), F32)
    dq, dk, dv = pl.pallas_call(
        attend_kernel,
        out_shape=(heads(2), acc, acc),
        in_specs=vmem_specs(5),
        out_specs=tuple(vmem_specs(3)),
        scratch_shapes=[vm((4, TC, TOK, PAD_DIM), BF16)] * 2 + [vm((TC + 2, TOK, 2 * TOK), F32)] * 2,
        name="attend",
    )(qh, gh, kh, vh, mask)
    img = sds((2, 64, D), BF16)
    piece = vm((16, TOK), F32)
    gq, gk, gv, gc, gw = pl.pallas_call(
        gather_kernel,
        out_shape=(img, img, img, img, sds((3, 3, D), F32)),
        in_specs=vmem_specs(5),
        out_specs=tuple(vmem_specs(5)),
        scratch_shapes=[vm((2, 2, TC, PAD_DIM, TOK), BF16)] * 2
        + [vm((2, TC, PAD_DIM, TOK), BF16)] * 2
        + [vm((HEADS, PAD_DIM, TOK), BF16)] * 3
        + [vm((D, TOK), F32), vm((4, 80, D), F32)]
        + [vm((2, 64, D), BF16), vm((2, 2, 16, D), BF16), vm((4, 16, D), BF16)]
        + [vm((TC, 16, TOK), F32), vm((TC, 16, TOK), F32), vm((NX, 16, TOK), F32), vm((NZ, 16, TOK), F32), vm((TC, 16, TOK), F32)]
        + [piece] * 3
        + [sem((2, 2)), sem((2, 2)), sem((3, HEADS)), sem((3,)), sem((8,)), sem((8,)), sem((4, 8)), sem((4,))],
        compiler_params=pltpu.CompilerParams(collective_id=1, has_side_effects=True),
        name="gather",
    )(dq, dk, dv, cext, kernel)
    return gq, gk, gv, gc, gw


def solution(mesh):
    tile = P("trow", "tcol", None)
    return jax.shard_map(
        per_device,
        mesh=mesh,
        in_specs=(tile, tile, tile, tile, P(), tile, P("trow", None, None)),
        out_specs=(tile, tile, tile, tile, P()),
        check_vma=False,
    )
```

time: 373 us -> 103 us (0.28); the launches traced: 366 us -> 103 us
  local copies, waits for them, and re-layouts: 108 us -> 5.51 us
  Pallas kernels: 0 us -> 96.6 us
  blocking collectives: 94 us -> 0 us
  matrix products: 60.8 us -> 0 us
  starting transfers between devices: 59.1 us -> 0 us
  other arithmetic: 26.9 us -> 0 us
  between operations: 15.5 us -> 0.68 us
    pallas_call x0 -> x3, Pallas kernels: none -> 96.6 us  [the longest x1 44.9 us: per_device(): pl.pallas_call(gather_kernel, out_shape=(img, img, img, img, sds((3, 3, D...]
    psum x1 -> x0, blocking collectives: 94 us -> none  [per_device(): grad_kernel = lax.psum(jnp.stack(kernel_rows, axis=0), ('trow', 'tcol'))]
    ppermute x16 -> x0, starting transfers between devices: 49.2 us -> none  [the longest x8 25 us: from_behind(): return lax.ppermute(shard, axis, pairs)]
    dot_general x22 -> x0, matrix products: 46.9 us -> none  [the longest x4 13 us: attend_group(): jnp.einsum('hqk,qhd->khd', grad_scores_bf, queries, preferred_element_typ...]
    slice x20 -> x0, local copies, waits for them, and re-layouts: 31.5 us -> none  [the longest x5 9.55 us: per_device(): all_values[:, low:high].reshape(-1, head_group, HEAD_DIM)]
    reshape x9 -> x0, local copies, waits for them, and re-layouts: 21.7 us -> none  [the longest x4 11.4 us: per_device(): value_parts.append(grad_v.reshape(-1, col_span))]
    concatenate x7 -> x0, local copies, waits for them, and re-layouts: 19.2 us -> none  [the longest x1 8.86 us: per_device(): grad_v_all = jnp.concatenate(value_parts, axis=1)]
    convert_element_type x10 -> x0, other arithmetic: 14.5 us -> none  [the longest x4 7.93 us: attend_group(): weights_bf = weights.astype(jnp.bfloat16)]
  transfers between devices with their start and end apart: 20 -> 0, of which waited for: 1 -> 0; matrix products, arithmetic and copies ran while one was open for 51% -> 0% of each run, Pallas kernels for 0% -> 0%
where the time goes in v1:
time: 103 us
  Pallas kernels  96.6 us (94%)
  local copies, waits for them, and re-layouts  5.51 us (5%)
    pallas_call x1, Pallas kernels, per_device(): pl.pallas_call(gather_kernel, out_shape=(img, img, img, img, sds((3, 3, D...  44.9 us
    pallas_call x1, Pallas kernels, per_device(): pl.pallas_call(scatter_kernel, out_shape=(heads(2), heads(2), heads(4), h...  33.2 us
    pallas_call x1, Pallas kernels, per_device(): pl.pallas_call(attend_kernel, out_shape=(heads(2), acc, acc), in_specs=vm...  18.6 us
    unnamed x11, local copies, waits for them, and re-layouts  5.51 us

profile of v1, /device:TPU:1, one launch (start us, length us, event | category | flops | bytes accessed | tf_op | source)
XLA Modules:
  0.0 102.8 jit_solution(10559257306159501413)
XLA Ops:
  0.6 33.2 %scatter.1 = (bf16[2,8,80,128]{3,2,1,0:T(8,128)(2,1)}, bf16[2,8,80,128]{3,2,1,0:T(8,128)(2,1)}, bf16[4,8,80,128]{3,2,1,0:T(8,128)(2,1)}, bf16[4,8,80,128]{3,2,1,...) custom-call(bf16[2,64,1152]{2,1,0:T(8,128)(2,1)} %q.1, bf16[2,64,1152]{2,1,0:T(8,128)(2,1)} %k.1, ...), custom_call_target="tpu_custom_call" | custom-call | tf_op jit(solution)/shard_map/scatter/pallas_call | solution.py:484
  33.8 18.6 %attend.1 = (bf16[2,8,80,128]{3,2,1,0:T(8,128)(2,1)}, f32[4,8,80,128]{3,2,1,0:T(8,128)}, f32[4,8,80,128]{3,2,1,0:T(8,128)}) custom-call(bf16[2,8,80,128]{3,2,1,0:T(8,128)(2,1)} %get-tuple-element.14.q, bf16[2,8,80,128]{3,2,1,0:T(8,128)(2,1)} %get-tuple-element.15.g, bf16[4,8,80,128]{3,2,1,0:T(8,128)(2,1)} %get-tuple-element.16.k, ...), custom_call_target="tpu_custom_call" | custom-call | tf_op jit(solution)/shard_map/attend/pallas_call | solution.py:497
  52.4 44.9 %gather.1 = (bf16[2,64,1152]{2,1,0:T(8,128)(2,1)}, bf16[2,64,1152]{2,1,0:T(8,128)(2,1)}, bf16[2,64,1152]{2,1,0:T(8,128)(2,1)}, bf16[2,64,1152]{2,1,0:T(8,128)(2,1)}, f32[3,3,1152]{2,1,0:T(4,128)}) custom-call(bf16[2,8,80,128]{3,2,1,0:T(8,128)(2,1)} %get-tuple-element.19.dq, f32[4,8,80,128]{3,2,1,0:T(8,128)} %get-tuple-element.20.dk, ...), custom_call_target="tpu_custom_call" | custom-call | tf_op jit(solution)/shard_map/gather/pallas_call | solution.py:507
  97.3 0.0 copy-start.1
  97.3 0.0 copy-start
  97.3 0.0 copy-start.2
  97.3 1.8 %copy.17 = bf16[2,64,1152]{2,1,0:T(8,128)(2,1)} copy(bf16[2,64,1152]{2,1,0:T(8,128)(2,1)} %get-tuple-element.28) | data formatting | bytes 589824
  99.1 1.7 %copy.18 = bf16[2,64,1152]{2,1,0:T(8,128)(2,1)} copy(bf16[2,64,1152]{2,1,0:T(8,128)(2,1)} %get-tuple-element.29) | data formatting | bytes 589824
  100.8 0.0 copy-done.1
  100.8 0.7 copy.19
  101.5 0.0 copy-done
  101.5 0.7 copy.20
  102.2 0.0 copy-done.2
  102.2 0.6 copy.21
Async XLA Ops:
  97.3 3.5 %copy-start.1 = (bf16[2,64,1152]{2,1,0:T(8,128)(2,1)S(1)}, bf16[2,64,1152]{2,1,0:T(8,128)(2,1)}, u32[]{:S(2)}) copy-start(bf16[2,64,1152]{2,1,0:T(8,128)(2,1)} %get-tuple-element.30) | copy-start | bytes 884740
  97.3 4.2 %copy-start = (bf16[2,64,1152]{2,1,0:T(8,128)(2,1)S(1)}, bf16[2,64,1152]{2,1,0:T(8,128)(2,1)}, u32[]{:S(2)}) copy-start(bf16[2,64,1152]{2,1,0:T(8,128)(2,1)} %get-tuple-element.31) | copy-start | bytes 884740
  97.3 4.9 %copy-start.2 = (f32[3,3,1152]{2,1,0:T(4,128)S(1)}, f32[3,3,1152]{2,1,0:T(4,128)}, u32[]{:S(2)}) copy-start(f32[3,3,1152]{2,1,0:T(4,128)} %get-tuple-element.32) | copy-start | bytes 124420

commit v2 on v1

v2 whole, which is shorter than its diff:
```python
import functools
import math

import jax
import jax.numpy as jnp
from jax import lax
from jax.experimental import pallas as pl
from jax.experimental.pallas import tpu as pltpu
from jax.sharding import PartitionSpec as P

HEADS = 16
HEAD_DIM = 72
PAD_DIM = 80
D = 1152
TOK = 128
NX = 4
NY = 4
TR = 32
TC = 8
NZ = TR // NX
LANES = D // 128
ROOT = HEAD_DIM ** (-0.5)
EXP_SCALE = ROOT * math.log2(math.e)
BIG = 1e30
MESH = pl.DeviceIdType.MESH
F32 = jnp.float32
BF16 = jnp.bfloat16
DIRS = ((-1, -1), (-1, 0), (-1, 1), (0, -1), (0, 1), (1, -1), (1, 0), (1, 1))


class Place:
    def __init__(self):
        self.tr = lax.axis_index("trow")
        self.tc = lax.axis_index("tcol")
        self.z = self.tr // NX
        self.x = self.tr % NX
        self.y = self.tc // 2
        self.c = self.tc % 2
        self.u = 2 * self.z + self.c

    def chain(self, step):
        u = self.u + step
        return (NX * (u // 2) + self.x, 2 * self.y + u % 2)

    def has_chain(self, step):
        u = self.u + step
        return (u >= 0) & (u < 2 * NZ)

    def has_dir(self, dr, dc):
        r = self.tr + dr
        c = self.tc + dc
        return (r >= 0) & (r < TR) & (c >= 0) & (c < TC)


def signal(sem, dev):
    pl.semaphore_signal(sem, inc=1, device_id=dev, device_id_type=MESH)


def greet(me):
    bar = pltpu.get_barrier_semaphore()
    total = jnp.int32(NX * TC - 1)
    for step in range(1, NX * TC):
        rank = (me.x * TC + me.tc + step) % (NX * TC)
        signal(bar, (NX * me.z + rank // TC, rank % TC))
    for step in (-1, 1):
        ok = me.has_chain(step)
        total = total + ok.astype(jnp.int32)

        @pl.when(ok)
        def _():
            signal(bar, me.chain(step))

    for dr, dc in DIRS:
        ok = me.has_dir(dr, dc)
        total = total + ok.astype(jnp.int32)

        @pl.when(ok)
        def _():
            signal(bar, (me.tr + dr, me.tc + dc))

    for step in range(1, NZ):
        signal(bar, (NX * ((me.z + step) % NZ) + me.x, me.tc))
    return bar, total + (NZ - 1)


def remote(src, dst, ssem, rsem, dev):
    return pltpu.make_async_remote_copy(
        src_ref=src, dst_ref=dst, send_sem=ssem, recv_sem=rsem, device_id=dev, device_id_type=MESH
    )


def start_or_local(is_self, src, dst, ssem, rsem, dev):
    @pl.when(is_self)
    def _():
        pltpu.make_async_copy(src, dst, rsem).start()

    @pl.when(jnp.logical_not(is_self))
    def _():
        remote(src, dst, ssem, rsem, dev).start()


def wait_sent(is_self, src, dst, ssem, rsem, dev):
    @pl.when(jnp.logical_not(is_self))
    def _():
        remote(src, dst, ssem, rsem, dev).wait_send()


def wait_bytes(ref, sem):
    pltpu.make_async_copy(ref, ref, sem).wait()


def halo_views(img, rows, cols, diag, dr, dc):
    row = 0 if dr < 0 else 1
    col = 0 if dc < 0 else 48
    if dc == 0:
        return img.at[row], rows.at[1 if dr < 0 else 0]
    if dr == 0:
        return img.at[:, pl.ds(col, 16), :], cols.at[1 if dc < 0 else 0]
    slot = (2 if dr < 0 else 0) + (1 if dc < 0 else 0)
    return img.at[row, pl.ds(col, 16), :], diag.at[slot]


def halo_start(me, img, rows, cols, diag, ssem, rsem):
    for at, (dr, dc) in enumerate(DIRS):
        src, dst = halo_views(img, rows, cols, diag, dr, dc)

        @pl.when(me.has_dir(dr, dc))
        def _():
            remote(src, dst, ssem.at[at], rsem.at[at], (me.tr + dr, me.tc + dc)).start()


def halo_wait(me, img, rows, cols, diag, ssem, rsem):
    for at, (dr, dc) in enumerate(DIRS):
        src, dst = halo_views(img, rows, cols, diag, dr, dc)

        @pl.when(me.has_dir(dr, dc))
        def _():
            remote(src, dst, ssem.at[at], rsem.at[at], (me.tr + dr, me.tc + dc)).wait_send()

        @pl.when(me.has_dir(-dr, -dc))
        def _():
            remote(src, dst, ssem.at[at], rsem.at[at], (me.tr - dr, me.tc - dc)).wait_recv()


def fill_ext(me, ext, img, rows, cols, diag):
    ext[1:3, 8:72, :] = img[...].astype(F32)
    up = me.has_dir(-1, 0)
    down = me.has_dir(1, 0)
    left = me.has_dir(0, -1)
    right = me.has_dir(0, 1)

    def put(ok, place, value):
        ext[place] = jnp.where(ok, value.astype(F32), 0.0)

    put(up, (0, slice(8, 72)), rows[0])
    put(down, (3, slice(8, 72)), rows[1])
    for r in range(2):
        put(left, (1 + r, slice(0, 8)), cols[0, r].astype(F32)[8:16])
        put(right, (1 + r, slice(72, 80)), cols[1, r].astype(F32)[0:8])
    put(up & left, (0, slice(0, 8)), diag[0].astype(F32)[8:16])
    put(up & right, (0, slice(72, 80)), diag[1].astype(F32)[0:8])
    put(down & left, (3, slice(0, 8)), diag[2].astype(F32)[8:16])
    put(down & right, (3, slice(72, 80)), diag[3].astype(F32)[0:8])


def to_heads(x, flip, out):
    for b in range(LANES):
        flip[pl.ds(b * 128, 128), :] = x(b).T
    zero = jnp.zeros((PAD_DIM - HEAD_DIM, TOK), F32)
    for h in range(HEADS):
        out[h] = jnp.concatenate([flip[pl.ds(h * HEAD_DIM, HEAD_DIM), :], zero], axis=0).astype(BF16)


def dot(a, b, ca, cb):
    return lax.dot_general(a, b, (((ca,), (cb,)), ((), ())), preferred_element_type=F32)


def from_heads(land, flip, put):
    for h in range(HEADS):
        flip[pl.ds(h * HEAD_DIM, HEAD_DIM), :] = land[h].astype(F32)[:HEAD_DIM]
    for b in range(LANES):
        put(b, flip[pl.ds(b * 128, 128), :].T)


def whole_kernel(
    q, k, v, g, c, w, db,
    oq, ok, ov, oc, ow,
    hq, hg, hk, hv, hm,
    sq, sg, sk, sv, sm, flip, ext, cext, hrow, hcol, hdiag, grow, gcol, gdiag,
    kt, vt, s_buf, t_buf, acc_k, acc_v, tq, tk, tv, edge, elan, lq, lk, lv,
    pieces, red1, red2, red3, red4, part2, part3, part4,
    asend, arecv, msend, mrecv, bsend, brecv, hsend, hrecv, gsend, grecv,
    esend, erecv, dsend, drecv, psend, precv,
):
    me = Place()
    bar, expected = greet(me)

    def raw(x):
        return lambda b: x[:, :, b * 128 : b * 128 + 128].reshape(TOK, 128).astype(F32)

    for p in range(TC):
        live = (db[0, me.tc, p] >= 0) | (me.tc == p)
        sm[pl.ds(p, 1), :] = jnp.full((1, TOK), jnp.where(live, 0.0, BIG), F32)
    to_heads(raw(k), flip, sk)
    pieces[...] = jnp.zeros(pieces.shape, F32)
    pl.semaphore_wait(bar, expected)
    halo_start(me, c, hrow, hcol, hdiag, hsend, hrecv)
    r_mine = me.x % 2

    def dest(h):
        dev = (NX * me.z + h // NY, 2 * (h % NY) + me.x // 2)
        return dev, (dev[0] == me.tr) & (dev[1] == me.tc)

    def head_copies(act, n, src, dst):
        for h in range(HEADS):
            dev, is_self = dest(h)
            act(is_self, src.at[h], dst.at[r_mine, me.tc], asend.at[n, h], arecv.at[n, r_mine], dev)

    def mask_copies(act):
        for h in range(HEADS):
            dev, is_self = dest(h)
            act(is_self, sm, hm.at[r_mine, me.tc], msend.at[h], mrecv, dev)

    own_k = hk.at[pl.ds(1, 2)]
    own_v = hv.at[pl.ds(1, 2)]
    head_copies(start_or_local, 0, sk, own_k)
    mask_copies(start_or_local)
    to_heads(raw(q), flip, sq)
    head_copies(start_or_local, 1, sq, hq)
    halo_wait(me, c, hrow, hcol, hdiag, hsend, hrecv)
    fill_ext(me, cext, c, hrow, hcol, hdiag)

    def v_block(b):
        lanes = slice(b * 128, b * 128 + 128)
        total = v[:, :, lanes].astype(F32)
        for a in range(3):
            for s in range(3):
                total = total + w[a, s, lanes][None, None, :] * cext[a : a + 2, 7 + s : 71 + s, lanes]
        return total.astype(BF16).astype(F32).reshape(TOK, 128)

    to_heads(v_block, flip, sv)
    head_copies(start_or_local, 2, sv, own_v)
    to_heads(raw(g), flip, sg)
    head_copies(start_or_local, 3, sg, hg)

    def row_copy(at, arr, buf, step):
        src, dst = (buf.at[1], buf.at[3]) if step < 0 else (buf.at[2], buf.at[0])
        return remote(src, dst, bsend.at[arr, at], brecv.at[arr, at], me.chain(step))

    def flip_row(src, out, a):
        def one(j, _):
            out[a, j] = src[a, j].astype(F32).T.astype(BF16)
            return 0

        lax.fori_loop(0, TC, one, 0)

    for n, arr, buf, out in ((0, 0, hk, kt), (2, 1, hv, vt)):
        for at, step in enumerate((-1, 1)):
            wait_bytes(buf.at[1 + at], arecv.at[n, at])

            @pl.when(me.has_chain(step))
            def _():
                row_copy(at, arr, buf, step).start()

        @pl.when(jnp.logical_not(me.has_chain(-1)))
        def _():
            buf[0] = jnp.zeros(buf.shape[1:], BF16)

        @pl.when(jnp.logical_not(me.has_chain(1)))
        def _():
            buf[3] = jnp.zeros(buf.shape[1:], BF16)

        for a in (1, 2):
            flip_row(buf, out, a)
    for n, buf in ((1, hq), (3, hg)):
        for at in range(2):
            wait_bytes(buf.at[at], arecv.at[n, at])
    wait_bytes(hm, mrecv)

    head = me.x * NY + me.y
    acc_k[...] = jnp.zeros(acc_k.shape, F32)
    acc_v[...] = jnp.zeros(acc_v.shape, F32)

    def tile_copy(act, n, src, land, r, j):
        dev = (NX * me.z + 2 * me.c + r, j)
        is_self = (dev[0] == me.tr) & (me.tc == j)
        act(is_self, src.at[r, j], land.at[head], dsend.at[n, r, j], drecv.at[n], dev)

    def edge_copy(arr, r, pair, step):
        view = pl.ds(2 * pair, 2)
        return remote(
            edge.at[arr, r, view], elan.at[arr, 1 - r, view],
            esend.at[arr, r, pair], erecv.at[arr, r], me.chain(step),
        )

    def visit(r, pair):
        j = 2 * pair
        step = 2 * r - 1
        qs = [hq[r, j], hq[r, j + 1]]
        gs = [hg[r, j], hg[r, j + 1]]
        q2 = jnp.concatenate(qs, axis=1)
        g2 = jnp.concatenate(gs, axis=1)
        bias = []
        for p in range(TC):
            bias.append(jnp.concatenate([hm[r, j, pl.ds(p, 1), :], hm[r, j + 1, pl.ds(p, 1), :]], axis=1))
        outer = jnp.full((1, 2 * TOK), jnp.where(me.has_chain(step), 0.0, BIG), F32)
        inner = jnp.zeros((1, 2 * TOK), F32)
        bias.extend([outer, inner] if r == 0 else [inner, outer])
        top = jnp.full((8, 2 * TOK), -3.0e38, F32)
        for p in range(TC + 2):
            if p < TC:
                s = dot(kt[1 + r, p], q2, 1, 0)
            else:
                a = r + 2 * (p - TC)
                s = jnp.concatenate([dot(kt[a, j + t], qs[t], 1, 0) for t in range(2)], axis=1)
            s_buf[p] = s
            top = jnp.maximum(top, jnp.max(s.reshape(TOK // 8, 8, 2 * TOK), axis=0) - bias[p])
        top = jnp.max(top, axis=0, keepdims=True) * EXP_SCALE
        total = jnp.zeros((8, 2 * TOK), F32)
        delta = jnp.zeros((8, 2 * TOK), F32)
        for p in range(TC + 2):
            e = jnp.exp2(s_buf[p] * EXP_SCALE - (top + bias[p]))
            if p < TC:
                gw = dot(vt[1 + r, p], g2, 1, 0)
            else:
                a = r + 2 * (p - TC)
                gw = jnp.concatenate([dot(vt[a, j + t], gs[t], 1, 0) for t in range(2)], axis=1)
            te = e * gw
            s_buf[p] = e
            t_buf[p] = te
            total = total + jnp.sum(e.reshape(TOK // 8, 8, 2 * TOK), axis=0)
            delta = delta + jnp.sum(te.reshape(TOK // 8, 8, 2 * TOK), axis=0)
        inv = 1.0 / jnp.sum(total, axis=0, keepdims=True)
        delta = jnp.sum(delta, axis=0, keepdims=True) * inv
        qn = (q2.astype(F32) * (inv * ROOT)).astype(BF16)
        gn = (g2.astype(F32) * inv).astype(BF16)
        dq = jnp.zeros((PAD_DIM, 2 * TOK), F32)
        for p in range(TC + 2):
            e = s_buf[p]
            ds = (t_buf[p] - e * delta).astype(BF16)
            eb = e.astype(BF16)
            if p < TC:
                dq = dq + dot(hk[1 + r, p], ds, 1, 0)
                acc_k[r, p] += dot(qn, ds, 1, 1)
                acc_v[r, p] += dot(gn, eb, 1, 1)
            else:
                a = r + 2 * (p - TC)
                parts = []
                for t in range(2):
                    half = slice(t * TOK, (t + 1) * TOK)
                    parts.append(dot(hk[a, j + t], ds[:, half], 1, 0))
                    key_term = dot(qn[:, half], ds[:, half], 1, 1)
                    value_term = dot(gn[:, half], eb[:, half], 1, 1)
                    if a in (0, 3):
                        edge[0, r, j + t] = key_term.astype(BF16)
                        edge[1, r, j + t] = value_term.astype(BF16)
                    else:
                        acc_k[1 - r, j + t] += key_term
                        acc_v[1 - r, j + t] += value_term
                dq = dq + jnp.concatenate(parts, axis=1)
        dq = (dq * (inv * ROOT)).astype(BF16)
        tq[r, j] = dq[:, :TOK]
        tq[r, j + 1] = dq[:, TOK:]

        @pl.when(me.has_chain(step))
        def _():
            edge_copy(1, r, pair, step).start()
            edge_copy(0, r, pair, step).start()

        for t in range(2):
            tile_copy(start_or_local, 0, tq, lq, r, j + t)

    for r, step in enumerate((-1, 1)):
        for arr, buf in ((0, hk), (1, hv)):

            @pl.when(me.has_chain(step))
            def _():
                row_copy(1 - r, arr, buf, -step).wait_recv()

        flip_row(hk, kt, 3 * r)
        flip_row(hv, vt, 3 * r)

        def body(pair, _):
            visit(r, pair)
            return 0

        lax.fori_loop(0, TC // 2, body, 0)

    for r, step in ((1, 1), (0, -1)):
        for arr, n, acc, out, land in ((1, 2, acc_v, tv, lv), (0, 1, acc_k, tk, lk)):

            @pl.when(me.has_chain(step))
            def _():
                wait_bytes(elan.at[arr, r], erecv.at[arr, 1 - r])

            extra = jnp.where(me.has_chain(step), elan[arr, r].astype(F32), 0.0)
            out[r] = (acc[r] + extra).astype(BF16)
            for j in range(TC):
                tile_copy(start_or_local, n, out, land, r, j)

    def out_block(out):
        def put(b, x):
            out[:, :, b * 128 : b * 128 + 128] = x.reshape(2, 64, 128).astype(BF16)

        return put

    wait_bytes(lq, drecv.at[0])
    from_heads(lq, flip, out_block(oq))
    wait_bytes(lv, drecv.at[2])
    from_heads(lv, flip, out_block(ov))
    halo_start(me, ov, grow, gcol, gdiag, gsend, grecv)
    for b in range(LANES):
        lanes = slice(b * 128, b * 128 + 128)
        gv = ov[:, :, lanes].astype(F32)
        for a in range(3):
            for s in range(3):
                prod = gv * cext[a : a + 2, 7 + s : 71 + s, lanes]
                t = (a * 3 + s) * LANES + b
                pieces[t // 11, pl.ds(t % 11, 1), :] = jnp.sum(prod.reshape(TOK, 128), axis=0, keepdims=True)

    def exchange(stage, count, mine, src, land, dev):
        def run(act):
            for other in range(count):
                view = src.at[other] if stage == 0 else src
                act(mine == other, view, land.at[mine], psend.at[stage, other], precv.at[stage], dev(other))

        run(start_or_local)
        return run

    runs = []
    runs.append(exchange(0, TC, me.tc, pieces, red1, lambda o: (me.tr, o)))
    wait_bytes(lk, drecv.at[1])
    from_heads(lk, flip, out_block(ok))
    wait_bytes(red1, precv.at[0])
    part2[...] = jnp.sum(red1[...], axis=0)
    runs.append(exchange(1, NX, me.x, part2, red2, lambda o: (NX * me.z + o, me.tc)))
    halo_wait(me, ov, grow, gcol, gdiag, gsend, grecv)
    fill_ext(me, ext, ov, grow, gcol, gdiag)
    wait_bytes(red2, precv.at[1])
    part3[...] = jnp.sum(red2[...], axis=0)
    runs.append(exchange(2, NZ, me.z, part3, red3, lambda o: (NX * o + me.x, me.tc)))
    for b in range(LANES):
        lanes = slice(b * 128, b * 128 + 128)
        total = jnp.zeros((2, 64, 128), F32)
        for a in range(3):
            for s in range(3):
                total = total + w[a, s, lanes][None, None, :] * ext[2 - a : 4 - a, 9 - s : 73 - s, lanes]
        oc[:, :, lanes] = total.astype(BF16)
    wait_bytes(red3, precv.at[2])
    part4[...] = jnp.sum(red3[...], axis=0)
    runs.append(exchange(3, TC, me.tc, part4, red4, lambda o: (me.tr, o)))

    for n, src, dst in ((0, sk, own_k), (1, sq, hq), (2, sv, own_v), (3, sg, hg)):
        head_copies(wait_sent, n, src, dst)
    mask_copies(wait_sent)
    for at, step in enumerate((-1, 1)):

        @pl.when(me.has_chain(step))
        def _():
            for arr, buf in ((0, hk), (1, hv)):
                row_copy(at, arr, buf, step).wait_send()
                for pair in range(TC // 2):
                    edge_copy(arr, at, pair, step).wait_send()

    for n, src, land in ((0, tq, lq), (1, tk, lk), (2, tv, lv)):
        for r in range(2):
            for j in range(TC):
                tile_copy(wait_sent, n, src, land, r, j)

    wait_bytes(red4, precv.at[3])
    for t in range(9 * LANES):
        tap, b = t // LANES, t % LANES
        ow[tap // 3, pl.ds(tap % 3, 1), b * 128 : b * 128 + 128] = red4[t // 11, pl.ds(t % 11, 1), :]
    for run in runs:
        run(wait_sent)


def copy_kernel(*refs):
    n = len(refs) // 2
    for src, dst in zip(refs[:n], refs[n:]):
        dst[...] = src[...]


def vmem_specs(n):
    return [pl.BlockSpec(memory_space=pltpu.VMEM)] * n


def per_device(query, key, value, control, kernel, grad_out, detail_blocks):
    sem = pltpu.SemaphoreType.DMA
    vm = pltpu.VMEM
    img = jax.ShapeDtypeStruct((2, 64, D), BF16)
    outs = (img, img, img, img, jax.ShapeDtypeStruct((3, 3, D), F32))
    rows = lambda n, t=BF16: vm((n, TC, PAD_DIM, TOK), t)
    tiles = vm((HEADS, PAD_DIM, TOK), BF16)
    halo = [vm((2, 64, D), BF16), vm((2, 2, 16, D), BF16), vm((4, 16, D), BF16)]
    reduced = lambda n: vm((n, 16, TOK), F32)
    results = pl.pallas_call(
        whole_kernel,
        out_shape=outs,
        in_specs=vmem_specs(6) + [pl.BlockSpec(memory_space=pltpu.SMEM)],
        out_specs=tuple(vmem_specs(5)),
        scratch_shapes=[rows(2), rows(2), rows(4), rows(4), vm((2, TC, 8, TOK), F32)]
        + [tiles] * 4
        + [vm((8, TOK), F32), vm((D, TOK), F32), vm((4, 80, D), F32), vm((4, 80, D), F32)]
        + halo
        + halo
        + [vm((4, TC, TOK, PAD_DIM), BF16)] * 2
        + [vm((TC + 2, TOK, 2 * TOK), F32)] * 2
        + [rows(2, F32)] * 2
        + [rows(2)] * 3
        + [vm((2, 2, TC, PAD_DIM, TOK), BF16)] * 2
        + [tiles] * 3
        + [reduced(TC), reduced(TC), reduced(NX), reduced(NZ), reduced(TC)]
        + [vm((16, TOK), F32)] * 3
        + [sem((4, HEADS)), sem((4, 2)), sem((HEADS,)), sem, sem((2, 2)), sem((2, 2))]
        + [sem((8,))] * 4
        + [sem((2, 2, 4)), sem((2, 2)), sem((3, 2, TC)), sem((3,)), sem((4, 8)), sem((4,))],
        compiler_params=pltpu.CompilerParams(collective_id=0, has_side_effects=True),
        name="whole",
    )(query, key, value, grad_out, control, kernel, detail_blocks)
    return pl.pallas_call(
        copy_kernel,
        out_shape=outs,
        in_specs=vmem_specs(5),
        out_specs=tuple(vmem_specs(5)),
        name="finish",
    )(*results)


def solution(mesh):
    tile = P("trow", "tcol", None)
    return jax.shard_map(
        per_device,
        mesh=mesh,
        in_specs=(tile, tile, tile, tile, P(), tile, P("trow", None, None)),
        out_specs=(tile, tile, tile, tile, P()),
        check_vma=False,
    )
```

time: 103 us -> 84.8 us (0.82)
  Pallas kernels: 96.6 us -> 84 us
  local copies, waits for them, and re-layouts: 5.51 us -> 0 us
    pallas_call x3 -> x2, Pallas kernels: 96.6 us -> 84 us  [the longest x1 81.7 us: per_device(): pl.pallas_call(whole_kernel, out_shape=outs, in_specs=vmem_specs(6) + [pl...]
    unnamed x11 -> x0, local copies, waits for them, and re-layouts: 5.51 us -> none
where the time goes in v2:
time: 84.8 us; the launch traced here: 84.6 us
  Pallas kernels  84 us (99%)
    pallas_call x1, Pallas kernels, per_device(): pl.pallas_call(whole_kernel, out_shape=outs, in_specs=vmem_specs(6) + [pl...  81.7 us
    pallas_call x1, Pallas kernels, per_device(): pl.pallas_call(copy_kernel, out_shape=outs, in_specs=vmem_specs(5), out_s...  2.27 us

profile of v2, /device:TPU:1, one launch (start us, length us, event | category | flops | bytes accessed | tf_op | source)
XLA Modules:
  0.0 84.6 jit_solution(2947024342300752221)
XLA Ops:
  0.6 81.7 %whole.1 = (bf16[2,64,1152]{2,1,0:T(8,128)(2,1)}, bf16[2,64,1152]{2,1,0:T(8,128)(2,1)}, bf16[2,64,1152]{2,1,0:T(8,128)(2,1)}, bf16[2,64,1152]{2,1,0:T(8,128)(2,1)}, f32[3,3,1152]{2,1,0:T(4,128)}) custom-call(bf16[2,64,1152]{2,1,0:T(8,128)(2,1)} %q.1, bf16[2,64,1152]{2,1,0:T(8,128)(2,1)} %k.1, bf16[2,64,1152]{2,1,0:T(8,128)(2,1)} %v.1, ...), custom_call_target="tpu_custom_call" | custom-call | tf_op jit(solution)/shard_map/whole/pallas_call | solution.py:497
  82.4 2.3 %finish.1 = (bf16[2,64,1152]{2,1,0:T(8,128)(2,1)}, bf16[2,64,1152]{2,1,0:T(8,128)(2,1)}, bf16[2,64,1152]{2,1,0:T(8,128)(2,1)}, bf16[2,64,1152]{2,1,0:T(8,128)(2,1)}, f32[3,3,1152]{2,1,0:T(4,128)}) custom-call(bf16[2,64,1152]{2,1,0:T(8,128)(2,1)} %get-tuple-element.10.refs_0_, bf16[2,64,1152]{2,1,0:T(8,128)(2,1)} %get-tuple-element.11.refs_1_, ...), custom_call_target="tpu_custom_call" | custom-call | tf_op jit(solution)/shard_map/finish/pallas_call | solution.py:521

commit v3 on v2

--- a/solution.py
+++ b/solution.py
@@ -109,29 +109,36 @@
     pltpu.make_async_copy(ref, ref, sem).wait()
 
 
-def halo_views(img, rows, cols, diag, dr, dc):
+def pack_rim(img, pack):
+    for side in range(2):
+        for r in range(2):
+            for b in range(LANES):
+                block = img[r, 48 * side : 48 * side + 16, b * 128 : b * 128 + 128].astype(F32)
+                pack[side, r, b : b + 1, :] = block[15 * side : 15 * side + 1]
+
+
+def halo_views(img, pack, rows, cols, diag, dr, dc):
     row = 0 if dr < 0 else 1
-    col = 0 if dc < 0 else 48
+    side = 0 if dc < 0 else 1
     if dc == 0:
         return img.at[row], rows.at[1 if dr < 0 else 0]
     if dr == 0:
-        return img.at[:, pl.ds(col, 16), :], cols.at[1 if dc < 0 else 0]
-    slot = (2 if dr < 0 else 0) + (1 if dc < 0 else 0)
-    return img.at[row, pl.ds(col, 16), :], diag.at[slot]
-
-
-def halo_start(me, img, rows, cols, diag, ssem, rsem):
+        return pack.at[side], cols.at[1 - side]
+    return pack.at[side, row], diag.at[(2 if dr < 0 else 0) + 1 - side]
+
+
+def halo_start(me, img, pack, rows, cols, diag, ssem, rsem):
     for at, (dr, dc) in enumerate(DIRS):
-        src, dst = halo_views(img, rows, cols, diag, dr, dc)
+        src, dst = halo_views(img, pack, rows, cols, diag, dr, dc)
 
         @pl.when(me.has_dir(dr, dc))
         def _():
             remote(src, dst, ssem.at[at], rsem.at[at], (me.tr + dr, me.tc + dc)).start()
 
 
-def halo_wait(me, img, rows, cols, diag, ssem, rsem):
+def halo_wait(me, img, pack, rows, cols, diag, ssem, rsem):
     for at, (dr, dc) in enumerate(DIRS):
-        src, dst = halo_views(img, rows, cols, diag, dr, dc)
+        src, dst = halo_views(img, pack, rows, cols, diag, dr, dc)
 
         @pl.when(me.has_dir(dr, dc))
         def _():
@@ -154,21 +161,25 @@
 
     put(up, (0, slice(8, 72)), rows[0])
     put(down, (3, slice(8, 72)), rows[1])
-    for r in range(2):
-        put(left, (1 + r, slice(0, 8)), cols[0, r].astype(F32)[8:16])
-        put(right, (1 + r, slice(72, 80)), cols[1, r].astype(F32)[0:8])
-    put(up & left, (0, slice(0, 8)), diag[0].astype(F32)[8:16])
-    put(up & right, (0, slice(72, 80)), diag[1].astype(F32)[0:8])
-    put(down & left, (3, slice(0, 8)), diag[2].astype(F32)[8:16])
-    put(down & right, (3, slice(72, 80)), diag[3].astype(F32)[0:8])
-
-
-def to_heads(x, flip, out):
+    for b in range(LANES):
+        lanes = slice(b * 128, b * 128 + 128)
+        piece = slice(b, b + 1)
+        for r in range(2):
+            put(left, (1 + r, slice(7, 8), lanes), cols[0, r, piece])
+            put(right, (1 + r, slice(72, 73), lanes), cols[1, r, piece])
+        put(up & left, (0, slice(7, 8), lanes), diag[0, piece])
+        put(up & right, (0, slice(72, 73), lanes), diag[1, piece])
+        put(down & left, (3, slice(7, 8), lanes), diag[2, piece])
+        put(down & right, (3, slice(72, 73), lanes), diag[3, piece])
+
+
+def to_heads(x, flip, out, tail=None):
     for b in range(LANES):
         flip[pl.ds(b * 128, 128), :] = x(b).T
-    zero = jnp.zeros((PAD_DIM - HEAD_DIM, TOK), F32)
+    if tail is None:
+        tail = jnp.zeros((PAD_DIM - HEAD_DIM, TOK), F32)
     for h in range(HEADS):
-        out[h] = jnp.concatenate([flip[pl.ds(h * HEAD_DIM, HEAD_DIM), :], zero], axis=0).astype(BF16)
+        out[h] = jnp.concatenate([flip[pl.ds(h * HEAD_DIM, HEAD_DIM), :], tail], axis=0).astype(BF16)
 
 
 def dot(a, b, ca, cb):
@@ -183,28 +194,36 @@
 
 
 def whole_kernel(
-    q, k, v, g, c, w, db,
+    q_hbm, k_hbm, v_hbm, g_hbm, c_hbm, w, db,
     oq, ok, ov, oc, ow,
-    hq, hg, hk, hv, hm,
-    sq, sg, sk, sv, sm, flip, ext, cext, hrow, hcol, hdiag, grow, gcol, gdiag,
-    kt, vt, s_buf, t_buf, acc_k, acc_v, tq, tk, tv, edge, elan, lq, lk, lv,
+    q, k, v, g, c,
+    hq, hg, hk, hv,
+    sq, sg, sk, sv, flip, ext, cext, cpack, hrow, hcol, hdiag, gpack, grow, gcol, gdiag,
+    kt, vt, s_buf, g_buf, e_buf, d_buf, top_buf, inv_buf, qn_buf, gn_buf,
+    acc_k, acc_v, tq, tk, tv, edge, elan, lq, lk, lv,
     pieces, red1, red2, red3, red4, part2, part3, part4,
-    asend, arecv, msend, mrecv, bsend, brecv, hsend, hrecv, gsend, grecv,
+    isem, asend, arecv, bsend, brecv, hsend, hrecv, gsend, grecv,
     esend, erecv, dsend, drecv, psend, precv,
 ):
     me = Place()
+    loads = [
+        pltpu.make_async_copy(src, dst, isem.at[at])
+        for at, (src, dst) in enumerate(((k_hbm, k), (c_hbm, c), (q_hbm, q), (v_hbm, v), (g_hbm, g)))
+    ]
+    for load in loads:
+        load.start()
     bar, expected = greet(me)
 
     def raw(x):
         return lambda b: x[:, :, b * 128 : b * 128 + 128].reshape(TOK, 128).astype(F32)
 
-    for p in range(TC):
-        live = (db[0, me.tc, p] >= 0) | (me.tc == p)
-        sm[pl.ds(p, 1), :] = jnp.full((1, TOK), jnp.where(live, 0.0, BIG), F32)
+    loads[0].wait()
     to_heads(raw(k), flip, sk)
+    loads[1].wait()
+    pack_rim(c, cpack)
     pieces[...] = jnp.zeros(pieces.shape, F32)
     pl.semaphore_wait(bar, expected)
-    halo_start(me, c, hrow, hcol, hdiag, hsend, hrecv)
+    halo_start(me, c, cpack, hrow, hcol, hdiag, hsend, hrecv)
     r_mine = me.x % 2
 
     def dest(h):
@@ -216,19 +235,21 @@
             dev, is_self = dest(h)
             act(is_self, src.at[h], dst.at[r_mine, me.tc], asend.at[n, h], arecv.at[n, r_mine], dev)
 
-    def mask_copies(act):
-        for h in range(HEADS):
-            dev, is_self = dest(h)
-            act(is_self, sm, hm.at[r_mine, me.tc], msend.at[h], mrecv, dev)
-
     own_k = hk.at[pl.ds(1, 2)]
     own_v = hv.at[pl.ds(1, 2)]
     head_copies(start_or_local, 0, sk, own_k)
-    mask_copies(start_or_local)
-    to_heads(raw(q), flip, sq)
+    loads[2].wait()
+    row_id = lax.broadcasted_iota(jnp.int32, (TC, TOK), 0)
+    dead = jnp.zeros((TC, TOK), F32)
+    for p in range(TC):
+        live = (db[0, me.tc, p] >= 0) | (me.tc == p)
+        dead = jnp.where(row_id == p, jnp.where(live, 0.0, BIG), dead)
+    to_heads(raw(q), flip, sq, dead)
     head_copies(start_or_local, 1, sq, hq)
-    halo_wait(me, c, hrow, hcol, hdiag, hsend, hrecv)
+    halo_wait(me, c, cpack, hrow, hcol, hdiag, hsend, hrecv)
     fill_ext(me, cext, c, hrow, hcol, hdiag)
+
+    loads[3].wait()
 
     def v_block(b):
         lanes = slice(b * 128, b * 128 + 128)
@@ -240,6 +261,7 @@
 
     to_heads(v_block, flip, sv)
     head_copies(start_or_local, 2, sv, own_v)
+    loads[4].wait()
     to_heads(raw(g), flip, sg)
     head_copies(start_or_local, 3, sg, hg)
 
@@ -248,11 +270,8 @@
         return remote(src, dst, bsend.at[arr, at], brecv.at[arr, at], me.chain(step))
 
     def flip_row(src, out, a):
-        def one(j, _):
+        for j in range(TC):
             out[a, j] = src[a, j].astype(F32).T.astype(BF16)
-            return 0
-
-        lax.fori_loop(0, TC, one, 0)
 
     for n, arr, buf, out in ((0, 0, hk, kt), (2, 1, hv, vt)):
         for at, step in enumerate((-1, 1)):
@@ -275,11 +294,8 @@
     for n, buf in ((1, hq), (3, hg)):
         for at in range(2):
             wait_bytes(buf.at[at], arecv.at[n, at])
-    wait_bytes(hm, mrecv)
 
     head = me.x * NY + me.y
-    acc_k[...] = jnp.zeros(acc_k.shape, F32)
-    acc_v[...] = jnp.zeros(acc_v.shape, F32)
 
     def tile_copy(act, n, src, land, r, j):
         dev = (NX * me.z + 2 * me.c + r, j)
@@ -293,84 +309,110 @@
             esend.at[arr, r, pair], erecv.at[arr, r], me.chain(step),
         )
 
-    def visit(r, pair):
-        j = 2 * pair
-        step = 2 * r - 1
+    def halves(t):
+        return slice(t * TOK, (t + 1) * TOK)
+
+    def scores(i):
+        r, j, par = i // 4, 2 * (i % 4), i % 2
         qs = [hq[r, j], hq[r, j + 1]]
         gs = [hg[r, j], hg[r, j + 1]]
         q2 = jnp.concatenate(qs, axis=1)
         g2 = jnp.concatenate(gs, axis=1)
-        bias = []
-        for p in range(TC):
-            bias.append(jnp.concatenate([hm[r, j, pl.ds(p, 1), :], hm[r, j + 1, pl.ds(p, 1), :]], axis=1))
-        outer = jnp.full((1, 2 * TOK), jnp.where(me.has_chain(step), 0.0, BIG), F32)
-        inner = jnp.zeros((1, 2 * TOK), F32)
-        bias.extend([outer, inner] if r == 0 else [inner, outer])
+        dead = q2[HEAD_DIM:].astype(F32)
+        far = jnp.where(me.has_chain(2 * r - 1), 0.0, BIG)
         top = jnp.full((8, 2 * TOK), -3.0e38, F32)
         for p in range(TC + 2):
             if p < TC:
-                s = dot(kt[1 + r, p], q2, 1, 0)
+                s_buf[par, p] = dot(kt[1 + r, p], q2, 1, 0)
+                g_buf[par, p] = dot(vt[1 + r, p], g2, 1, 0)
+                bias = dead[p : p + 1]
             else:
                 a = r + 2 * (p - TC)
-                s = jnp.concatenate([dot(kt[a, j + t], qs[t], 1, 0) for t in range(2)], axis=1)
-            s_buf[p] = s
-            top = jnp.maximum(top, jnp.max(s.reshape(TOK // 8, 8, 2 * TOK), axis=0) - bias[p])
-        top = jnp.max(top, axis=0, keepdims=True) * EXP_SCALE
+                for t in range(2):
+                    s_buf[par, p, :, halves(t)] = dot(kt[a, j + t], qs[t], 1, 0)
+                    g_buf[par, p, :, halves(t)] = dot(vt[a, j + t], gs[t], 1, 0)
+                bias = far if a in (0, 3) else 0.0
+            top = jnp.maximum(top, jnp.max(s_buf[par, p].reshape(TOK // 8, 8, 2 * TOK), axis=0) - bias)
+        top_buf[par] = top
+
+    def soften(i):
+        r, j, par = i // 4, 2 * (i % 4), i % 2
+        q2 = jnp.concatenate([hq[r, j], hq[r, j + 1]], axis=1).astype(F32)
+        g2 = jnp.concatenate([hg[r, j], hg[r, j + 1]], axis=1).astype(F32)
+        dead = q2[HEAD_DIM:]
+        far = jnp.where(me.has_chain(2 * r - 1), 0.0, BIG)
+        top = jnp.max(top_buf[par], axis=0, keepdims=True) * EXP_SCALE
         total = jnp.zeros((8, 2 * TOK), F32)
         delta = jnp.zeros((8, 2 * TOK), F32)
         for p in range(TC + 2):
-            e = jnp.exp2(s_buf[p] * EXP_SCALE - (top + bias[p]))
             if p < TC:
-                gw = dot(vt[1 + r, p], g2, 1, 0)
+                shift = top + dead[p : p + 1]
             else:
-                a = r + 2 * (p - TC)
-                gw = jnp.concatenate([dot(vt[a, j + t], gs[t], 1, 0) for t in range(2)], axis=1)
-            te = e * gw
-            s_buf[p] = e
-            t_buf[p] = te
+                shift = top + far if r + 2 * (p - TC) in (0, 3) else top
+            e = jnp.exp2(s_buf[par, p] * EXP_SCALE - shift)
+            s_buf[par, p] = e
+            e_buf[par, p] = e.astype(BF16)
             total = total + jnp.sum(e.reshape(TOK // 8, 8, 2 * TOK), axis=0)
-            delta = delta + jnp.sum(te.reshape(TOK // 8, 8, 2 * TOK), axis=0)
+            delta = delta + jnp.sum((e * g_buf[par, p]).reshape(TOK // 8, 8, 2 * TOK), axis=0)
         inv = 1.0 / jnp.sum(total, axis=0, keepdims=True)
         delta = jnp.sum(delta, axis=0, keepdims=True) * inv
-        qn = (q2.astype(F32) * (inv * ROOT)).astype(BF16)
-        gn = (g2.astype(F32) * inv).astype(BF16)
-        dq = jnp.zeros((PAD_DIM, 2 * TOK), F32)
         for p in range(TC + 2):
-            e = s_buf[p]
-            ds = (t_buf[p] - e * delta).astype(BF16)
-            eb = e.astype(BF16)
-            if p < TC:
-                dq = dq + dot(hk[1 + r, p], ds, 1, 0)
-                acc_k[r, p] += dot(qn, ds, 1, 1)
-                acc_v[r, p] += dot(gn, eb, 1, 1)
-            else:
+            d_buf[par, p] = (s_buf[par, p] * (g_buf[par, p] - delta)).astype(BF16)
+        scaled = inv * ROOT
+        inv_buf[par] = jnp.broadcast_to(scaled, (8, 2 * TOK))
+        qn_buf[par] = (q2 * scaled).astype(BF16)
+        gn_buf[par] = (g2 * inv).astype(BF16)
+
+    def grads(i):
+        r, j, par = i // 4, 2 * (i % 4), i % 2
+        qn = qn_buf[par]
+        gn = gn_buf[par]
+
+        def add(acc, at, tile, value, first):
+            acc[at, tile] = value if first else acc[at, tile] + value
+
+        ds_row = jnp.concatenate([d_buf[par, p] for p in range(TC)], axis=0)
+        e_row = jnp.concatenate([e_buf[par, p] for p in range(TC)], axis=0)
+        dq = dot(jnp.concatenate([hk[1 + r, p] for p in range(TC)], axis=1), ds_row, 1, 0)
+        key_row = dot(qn, ds_row, 1, 1)
+        value_row = dot(gn, e_row, 1, 1)
+        for p in range(TC):
+            add(acc_k, r, p, key_row[:, halves(p)], i == 0)
+            add(acc_v, r, p, value_row[:, halves(p)], i == 0)
+        parts = []
+        for t in range(2):
+            part = jnp.zeros((PAD_DIM, TOK), F32)
+            for p in range(TC, TC + 2):
                 a = r + 2 * (p - TC)
-                parts = []
-                for t in range(2):
-                    half = slice(t * TOK, (t + 1) * TOK)
-                    parts.append(dot(hk[a, j + t], ds[:, half], 1, 0))
-                    key_term = dot(qn[:, half], ds[:, half], 1, 1)
-                    value_term = dot(gn[:, half], eb[:, half], 1, 1)
-                    if a in (0, 3):
-                        edge[0, r, j + t] = key_term.astype(BF16)
-                        edge[1, r, j + t] = value_term.astype(BF16)
-                    else:
-                        acc_k[1 - r, j + t] += key_term
-                        acc_v[1 - r, j + t] += value_term
-                dq = dq + jnp.concatenate(parts, axis=1)
-        dq = (dq * (inv * ROOT)).astype(BF16)
+                ds = d_buf[par, p, :, halves(t)]
+                part = part + dot(hk[a, j + t], ds, 1, 0)
+                key_term = dot(qn[:, halves(t)], ds, 1, 1)
+                value_term = dot(gn[:, halves(t)], e_buf[par, p, :, halves(t)], 1, 1)
+                if a in (0, 3):
+                    edge[0, r, j + t] = key_term.astype(BF16)
+                    edge[1, r, j + t] = value_term.astype(BF16)
+                else:
+                    add(acc_k, 1 - r, j + t, key_term, r == 0)
+                    add(acc_v, 1 - r, j + t, value_term, r == 0)
+            parts.append(part)
+        dq = ((dq + jnp.concatenate(parts, axis=1)) * inv_buf[par, 0:1]).astype(BF16)
         tq[r, j] = dq[:, :TOK]
         tq[r, j + 1] = dq[:, TOK:]
 
+    def send_terms(i):
+        r, pair = i // 4, i % 4
+        step = 2 * r - 1
+
         @pl.when(me.has_chain(step))
         def _():
             edge_copy(1, r, pair, step).start()
             edge_copy(0, r, pair, step).start()
 
         for t in range(2):
-            tile_copy(start_or_local, 0, tq, lq, r, j + t)
-
-    for r, step in enumerate((-1, 1)):
+            tile_copy(start_or_local, 0, tq, lq, r, 2 * pair + t)
+
+    def take_outer(r):
+        step = 2 * r - 1
         for arr, buf in ((0, hk), (1, hv)):
 
             @pl.when(me.has_chain(step))
@@ -380,11 +422,20 @@
         flip_row(hk, kt, 3 * r)
         flip_row(hv, vt, 3 * r)
 
-        def body(pair, _):
-            visit(r, pair)
-            return 0
-
-        lax.fori_loop(0, TC // 2, body, 0)
+    visits = TC
+    take_outer(0)
+    scores(0)
+    for i in range(visits + 1):
+        if i + 1 == visits // 2:
+            take_outer(1)
+        if i >= 1:
+            grads(i - 1)
+        if i < visits:
+            soften(i)
+        if i + 1 < visits:
+            scores(i + 1)
+        if i >= 1:
+            send_terms(i - 1)
 
     for r, step in ((1, 1), (0, -1)):
         for arr, n, acc, out, land in ((1, 2, acc_v, tv, lv), (0, 1, acc_k, tk, lk)):
@@ -394,7 +445,8 @@
                 wait_bytes(elan.at[arr, r], erecv.at[arr, 1 - r])
 
             extra = jnp.where(me.has_chain(step), elan[arr, r].astype(F32), 0.0)
-            out[r] = (acc[r] + extra).astype(BF16)
+            for j in range(TC):
+                out[r, j] = (acc[r, j] + extra[j]).astype(BF16)
             for j in range(TC):
                 tile_copy(start_or_local, n, out, land, r, j)
 
@@ -408,7 +460,8 @@
     from_heads(lq, flip, out_block(oq))
     wait_bytes(lv, drecv.at[2])
     from_heads(lv, flip, out_block(ov))
-    halo_start(me, ov, grow, gcol, gdiag, gsend, grecv)
+    pack_rim(ov, gpack)
+    halo_start(me, ov, gpack, grow, gcol, gdiag, gsend, grecv)
     for b in range(LANES):
         lanes = slice(b * 128, b * 128 + 128)
         gv = ov[:, :, lanes].astype(F32)
@@ -434,7 +487,7 @@
     wait_bytes(red1, precv.at[0])
     part2[...] = jnp.sum(red1[...], axis=0)
     runs.append(exchange(1, NX, me.x, part2, red2, lambda o: (NX * me.z + o, me.tc)))
-    halo_wait(me, ov, grow, gcol, gdiag, gsend, grecv)
+    halo_wait(me, ov, gpack, grow, gcol, gdiag, gsend, grecv)
     fill_ext(me, ext, ov, grow, gcol, gdiag)
     wait_bytes(red2, precv.at[1])
     part3[...] = jnp.sum(red2[...], axis=0)
@@ -452,7 +505,6 @@
 
     for n, src, dst in ((0, sk, own_k), (1, sq, hq), (2, sv, own_v), (3, sg, hg)):
         head_copies(wait_sent, n, src, dst)
-    mask_copies(wait_sent)
     for at, step in enumerate((-1, 1)):
 
         @pl.when(me.has_chain(step))
@@ -492,27 +544,31 @@
     outs = (img, img, img, img, jax.ShapeDtypeStruct((3, 3, D), F32))
     rows = lambda n, t=BF16: vm((n, TC, PAD_DIM, TOK), t)
     tiles = vm((HEADS, PAD_DIM, TOK), BF16)
-    halo = [vm((2, 64, D), BF16), vm((2, 2, 16, D), BF16), vm((4, 16, D), BF16)]
+    halo = [vm((2, 2, 16, TOK), F32), vm((2, 64, D), BF16), vm((2, 2, 16, TOK), F32), vm((4, 16, TOK), F32)]
+    pair = lambda t: vm((2, TC + 2, TOK, 2 * TOK), t)
+    wide = vm((2, 8, 2 * TOK), F32)
     reduced = lambda n: vm((n, 16, TOK), F32)
     results = pl.pallas_call(
         whole_kernel,
         out_shape=outs,
-        in_specs=vmem_specs(6) + [pl.BlockSpec(memory_space=pltpu.SMEM)],
+        in_specs=[pl.BlockSpec(memory_space=pl.ANY)] * 5 + vmem_specs(1) + [pl.BlockSpec(memory_space=pltpu.SMEM)],
         out_specs=tuple(vmem_specs(5)),
-        scratch_shapes=[rows(2), rows(2), rows(4), rows(4), vm((2, TC, 8, TOK), F32)]
+        scratch_shapes=[vm((2, 64, D), BF16)] * 5
+        + [rows(2), rows(2), rows(4), rows(4)]
         + [tiles] * 4
-        + [vm((8, TOK), F32), vm((D, TOK), F32), vm((4, 80, D), F32), vm((4, 80, D), F32)]
+        + [vm((D, TOK), F32), vm((4, 80, D), F32), vm((4, 80, D), F32)]
         + halo
         + halo
         + [vm((4, TC, TOK, PAD_DIM), BF16)] * 2
-        + [vm((TC + 2, TOK, 2 * TOK), F32)] * 2
+        + [pair(F32), pair(F32), pair(BF16), pair(BF16), wide, wide]
+        + [vm((2, PAD_DIM, 2 * TOK), BF16)] * 2
         + [rows(2, F32)] * 2
         + [rows(2)] * 3
         + [vm((2, 2, TC, PAD_DIM, TOK), BF16)] * 2
         + [tiles] * 3
         + [reduced(TC), reduced(TC), reduced(NX), reduced(NZ), reduced(TC)]
         + [vm((16, TOK), F32)] * 3
-        + [sem((4, HEADS)), sem((4, 2)), sem((HEADS,)), sem, sem((2, 2)), sem((2, 2))]
+        + [sem((5,)), sem((4, HEADS)), sem((4, 2)), sem((2, 2)), sem((2, 2))]
         + [sem((8,))] * 4
         + [sem((2, 2, 4)), sem((2, 2)), sem((3, 2, TC)), sem((3,)), sem((4, 8)), sem((4,))],
         compiler_params=pltpu.CompilerParams(collective_id=0, has_side_effects=True),

time: 84.8 us -> 79.1 us (0.933)
  Pallas kernels: 84 us -> 78.3 us
    pallas_call x1, Pallas kernels: 81.7 us -> 76 us  [per_device(): pl.pallas_call(whole_kernel, out_shape=outs, in_specs=[pl.BlockSpec(memor...]
where the time goes in v3:
time: 79.1 us; the launch traced here: 78.9 us
  Pallas kernels  78.3 us (99%)
    pallas_call x1, Pallas kernels, per_device(): pl.pallas_call(whole_kernel, out_shape=outs, in_specs=[pl.BlockSpec(memor...  76 us
    pallas_call x1, Pallas kernels, per_device(): pl.pallas_call(copy_kernel, out_shape=outs, in_specs=vmem_specs(5), out_s...  2.27 us

profile of v3, /device:TPU:1, one launch (start us, length us, event | category | flops | bytes accessed | tf_op | source)
XLA Modules:
  0.0 78.9 jit_solution(4575189614384015027)
XLA Ops:
  0.6 76.0 %whole.1 = (bf16[2,64,1152]{2,1,0:T(8,128)(2,1)}, bf16[2,64,1152]{2,1,0:T(8,128)(2,1)}, bf16[2,64,1152]{2,1,0:T(8,128)(2,1)}, bf16[2,64,1152]{2,1,0:T(8,128)(2,1)}, f32[3,3,1152]{2,1,0:T(4,128)}) custom-call(bf16[2,64,1152]{2,1,0:T(8,128)(2,1)} %q_hbm.1, bf16[2,64,1152]{2,1,0:T(8,128)(2,1)} %k_hbm.1, bf16[2,64,1152]{2,1,0:T(8,128)(2,1)} %v_hbm.1, ...), custom_call_target="tpu_custom_call" | custom-call | tf_op jit(solution)/shard_map/whole/pallas_call | solution.py:551
  76.7 2.3 %finish.1 = (bf16[2,64,1152]{2,1,0:T(8,128)(2,1)}, bf16[2,64,1152]{2,1,0:T(8,128)(2,1)}, bf16[2,64,1152]{2,1,0:T(8,128)(2,1)}, bf16[2,64,1152]{2,1,0:T(8,128)(2,1)}, f32[3,3,1152]{2,1,0:T(4,128)}) custom-call(bf16[2,64,1152]{2,1,0:T(8,128)(2,1)} %get-tuple-element.10.refs_0_, bf16[2,64,1152]{2,1,0:T(8,128)(2,1)} %get-tuple-element.11.refs_1_, ...), custom_call_target="tpu_custom_call" | custom-call | tf_op jit(solution)/shard_map/finish/pallas_call | solution.py:577

commit v4 on v3

--- a/solution.py
+++ b/solution.py
@@ -197,11 +197,11 @@
     q_hbm, k_hbm, v_hbm, g_hbm, c_hbm, w, db,
     oq, ok, ov, oc, ow,
     q, k, v, g, c,
-    hq, hg, hk, hv,
-    sq, sg, sk, sv, flip, ext, cext, cpack, hrow, hcol, hdiag, gpack, grow, gcol, gdiag,
+    hq, hg, hk, hv, hc,
+    sq, sg, sk, sv, sc, flip, ext, cext, cpack, hrow, hcol, hdiag, gpack, grow, gcol, gdiag,
     kt, vt, s_buf, g_buf, e_buf, d_buf, top_buf, inv_buf, qn_buf, gn_buf,
     acc_k, acc_v, tq, tk, tv, edge, elan, lq, lk, lv,
-    pieces, red1, red2, red3, red4, part2, part3, part4,
+    taps, red1, red2, red3, part1, part2, part3,
     isem, asend, arecv, bsend, brecv, hsend, hrecv, gsend, grecv,
     esend, erecv, dsend, drecv, psend, precv,
 ):
@@ -221,7 +221,6 @@
     to_heads(raw(k), flip, sk)
     loads[1].wait()
     pack_rim(c, cpack)
-    pieces[...] = jnp.zeros(pieces.shape, F32)
     pl.semaphore_wait(bar, expected)
     halo_start(me, c, cpack, hrow, hcol, hdiag, hsend, hrecv)
     r_mine = me.x % 2
@@ -264,6 +263,9 @@
     loads[4].wait()
     to_heads(raw(g), flip, sg)
     head_copies(start_or_local, 3, sg, hg)
+    own_c = hc.at[pl.ds(1, 2)]
+    to_heads(raw(c), flip, sc)
+    head_copies(start_or_local, 4, sc, own_c)
 
     def row_copy(at, arr, buf, step):
         src, dst = (buf.at[1], buf.at[3]) if step < 0 else (buf.at[2], buf.at[0])
@@ -273,7 +275,7 @@
         for j in range(TC):
             out[a, j] = src[a, j].astype(F32).T.astype(BF16)
 
-    for n, arr, buf, out in ((0, 0, hk, kt), (2, 1, hv, vt)):
+    def pass_rows(n, arr, buf):
         for at, step in enumerate((-1, 1)):
             wait_bytes(buf.at[1 + at], arecv.at[n, at])
 
@@ -281,14 +283,12 @@
             def _():
                 row_copy(at, arr, buf, step).start()
 
-        @pl.when(jnp.logical_not(me.has_chain(-1)))
-        def _():
-            buf[0] = jnp.zeros(buf.shape[1:], BF16)
-
-        @pl.when(jnp.logical_not(me.has_chain(1)))
-        def _():
-            buf[3] = jnp.zeros(buf.shape[1:], BF16)
-
+            @pl.when(jnp.logical_not(me.has_chain(step)))
+            def _():
+                buf[3 * at] = jnp.zeros(buf.shape[1:], BF16)
+
+    for n, arr, buf, out in ((0, 0, hk, kt), (2, 1, hv, vt)):
+        pass_rows(n, arr, buf)
         for a in (1, 2):
             flip_row(buf, out, a)
     for n, buf in ((1, hq), (3, hg)):
@@ -436,9 +436,11 @@
             scores(i + 1)
         if i >= 1:
             send_terms(i - 1)
-
-    for r, step in ((1, 1), (0, -1)):
-        for arr, n, acc, out, land in ((1, 2, acc_v, tv, lv), (0, 1, acc_k, tk, lk)):
+        if i == 1:
+            pass_rows(4, 2, hc)
+
+    for arr, n, acc, out, land in ((1, 2, acc_v, tv, lv), (0, 1, acc_k, tk, lk)):
+        for r, step in ((1, 1), (0, -1)):
 
             @pl.when(me.has_chain(step))
             def _():
@@ -450,6 +452,62 @@
             for j in range(TC):
                 tile_copy(start_or_local, n, out, land, r, j)
 
+    for step in (-1, 1):
+
+        @pl.when(me.has_chain(step))
+        def _():
+            row_copy((1 - step) // 2, 2, hc, -step).wait_recv()
+
+    lane = lax.broadcasted_iota(jnp.int32, (PAD_DIM, TOK), 1)
+    low = lane < TOK // 2
+    first = lane % 64 == 0
+    last = lane % 64 == 63
+    blank = jnp.zeros((PAD_DIM, TOK), F32)
+    for a in range(3):
+        for r in range(2):
+            taps[a, r, 0] = blank
+            taps[a, r, TC + 1] = blank
+
+    def shift_rows(j, _):
+        for r in range(2):
+            own = hc[1 + r, j].astype(F32)
+            taps[0, r, j + 1] = pltpu.roll(jnp.where(low, own, hc[r, j].astype(F32)), 64, 1)
+            taps[1, r, j + 1] = own
+            taps[2, r, j + 1] = pltpu.roll(jnp.where(low, hc[2 + r, j].astype(F32), own), 64, 1)
+        return 0
+
+    lax.fori_loop(0, TC, shift_rows, 0)
+    table = blank
+    for a in range(3):
+
+        def add_tile(j, sums):
+            for r in range(2):
+                gv = tv[r, j].astype(F32)
+                here = taps[a, r, j + 1]
+                left = jnp.where(first, pltpu.roll(taps[a, r, j], 65, 1), pltpu.roll(here, 1, 1))
+                right = jnp.where(last, pltpu.roll(taps[a, r, j + 2], 63, 1), pltpu.roll(here, 127, 1))
+                sums = (sums[0] + left * gv, sums[1] + here * gv, sums[2] + right * gv)
+            return sums
+
+        sums = lax.fori_loop(0, TC, add_tile, (blank, blank, blank))
+        for b in range(3):
+            table = jnp.where(lane == 3 * a + b, jnp.sum(sums[b], axis=1, keepdims=True), table)
+    table = jnp.concatenate([table, jnp.zeros((TOK - PAD_DIM, TOK), F32)], axis=0)
+    part1[...] = table.T[:16]
+
+    def exchange(stage, count, mine, src, land, dev):
+        def run(act):
+            for other in range(count):
+                act(mine == other, src, land.at[mine], psend.at[stage, other], precv.at[stage], dev(other))
+
+        run(start_or_local)
+        return run
+
+    runs = [exchange(0, 2, me.c, part1, red1, lambda o: (me.tr, 2 * me.y + o))]
+
+    for n, src, dst in ((0, sk, own_k), (1, sq, hq), (2, sv, own_v), (3, sg, hg), (4, sc, own_c)):
+        head_copies(wait_sent, n, src, dst)
+
     def out_block(out):
         def put(b, x):
             out[:, :, b * 128 : b * 128 + 128] = x.reshape(2, 64, 128).astype(BF16)
@@ -458,40 +516,37 @@
 
     wait_bytes(lq, drecv.at[0])
     from_heads(lq, flip, out_block(oq))
+    wait_bytes(red1, precv.at[0])
+    part2[...] = jnp.sum(red1[...], axis=0)
+    runs.append(exchange(1, NZ, me.z, part2, red2, lambda o: (NX * o + me.x, me.tc)))
     wait_bytes(lv, drecv.at[2])
     from_heads(lv, flip, out_block(ov))
     pack_rim(ov, gpack)
     halo_start(me, ov, gpack, grow, gcol, gdiag, gsend, grecv)
-    for b in range(LANES):
-        lanes = slice(b * 128, b * 128 + 128)
-        gv = ov[:, :, lanes].astype(F32)
-        for a in range(3):
-            for s in range(3):
-                prod = gv * cext[a : a + 2, 7 + s : 71 + s, lanes]
-                t = (a * 3 + s) * LANES + b
-                pieces[t // 11, pl.ds(t % 11, 1), :] = jnp.sum(prod.reshape(TOK, 128), axis=0, keepdims=True)
-
-    def exchange(stage, count, mine, src, land, dev):
-        def run(act):
-            for other in range(count):
-                view = src.at[other] if stage == 0 else src
-                act(mine == other, view, land.at[mine], psend.at[stage, other], precv.at[stage], dev(other))
-
-        run(start_or_local)
-        return run
-
-    runs = []
-    runs.append(exchange(0, TC, me.tc, pieces, red1, lambda o: (me.tr, o)))
     wait_bytes(lk, drecv.at[1])
     from_heads(lk, flip, out_block(ok))
-    wait_bytes(red1, precv.at[0])
-    part2[...] = jnp.sum(red1[...], axis=0)
-    runs.append(exchange(1, NX, me.x, part2, red2, lambda o: (NX * me.z + o, me.tc)))
+    wait_bytes(red2, precv.at[1])
+    part3[...] = jnp.sum(red2[...], axis=0)
+    runs.append(
+        exchange(2, HEADS, head, part3, red3, lambda o: (NX * me.z + o // NY, 2 * (o % NY) + me.c))
+    )
+    for at, step in enumerate((-1, 1)):
+
+        @pl.when(me.has_chain(step))
+        def _():
+            for arr, buf in ((0, hk), (1, hv), (2, hc)):
+                row_copy(at, arr, buf, step).wait_send()
+            for arr in range(2):
+                for pair in range(TC // 2):
+                    edge_copy(arr, at, pair, step).wait_send()
+
+    for n, src, land in ((0, tq, lq), (1, tk, lk), (2, tv, lv)):
+        for r in range(2):
+            for j in range(TC):
+                tile_copy(wait_sent, n, src, land, r, j)
+
     halo_wait(me, ov, gpack, grow, gcol, gdiag, gsend, grecv)
     fill_ext(me, ext, ov, grow, gcol, gdiag)
-    wait_bytes(red2, precv.at[1])
-    part3[...] = jnp.sum(red2[...], axis=0)
-    runs.append(exchange(2, NZ, me.z, part3, red3, lambda o: (NX * o + me.x, me.tc)))
     for b in range(LANES):
         lanes = slice(b * 128, b * 128 + 128)
         total = jnp.zeros((2, 64, 128), F32)
@@ -499,30 +554,19 @@
             for s in range(3):
                 total = total + w[a, s, lanes][None, None, :] * ext[2 - a : 4 - a, 9 - s : 73 - s, lanes]
         oc[:, :, lanes] = total.astype(BF16)
+
     wait_bytes(red3, precv.at[2])
-    part4[...] = jnp.sum(red3[...], axis=0)
-    runs.append(exchange(3, TC, me.tc, part4, red4, lambda o: (me.tr, o)))
-
-    for n, src, dst in ((0, sk, own_k), (1, sq, hq), (2, sv, own_v), (3, sg, hg)):
-        head_copies(wait_sent, n, src, dst)
-    for at, step in enumerate((-1, 1)):
-
-        @pl.when(me.has_chain(step))
-        def _():
-            for arr, buf in ((0, hk), (1, hv)):
-                row_copy(at, arr, buf, step).wait_send()
-                for pair in range(TC // 2):
-                    edge_copy(arr, at, pair, step).wait_send()
-
-    for n, src, land in ((0, tq, lq), (1, tk, lk), (2, tv, lv)):
-        for r in range(2):
-            for j in range(TC):
-                tile_copy(wait_sent, n, src, land, r, j)
-
-    wait_bytes(red4, precv.at[3])
-    for t in range(9 * LANES):
-        tap, b = t // LANES, t % LANES
-        ow[tap // 3, pl.ds(tap % 3, 1), b * 128 : b * 128 + 128] = red4[t // 11, pl.ds(t % 11, 1), :]
+    column = lax.broadcasted_iota(jnp.int32, (16, TOK), 1)
+    blocks = [jnp.zeros((16, TOK), F32) for _ in range(LANES)]
+    for h in range(HEADS):
+        b, off = h * HEAD_DIM // 128, h * HEAD_DIM % 128
+        piece = pltpu.roll(red3[h], off, 1) if off else red3[h]
+        blocks[b] = blocks[b] + jnp.where(column >= off, piece, 0.0)
+        if off + HEAD_DIM > 128:
+            blocks[b + 1] = blocks[b + 1] + jnp.where(column < off, piece, 0.0)
+    for b in range(LANES):
+        for tap in range(9):
+            ow[tap // 3, tap % 3 : tap % 3 + 1, b * 128 : b * 128 + 128] = blocks[b][tap : tap + 1]
     for run in runs:
         run(wait_sent)
 
@@ -554,8 +598,8 @@
         in_specs=[pl.BlockSpec(memory_space=pl.ANY)] * 5 + vmem_specs(1) + [pl.BlockSpec(memory_space=pltpu.SMEM)],
         out_specs=tuple(vmem_specs(5)),
         scratch_shapes=[vm((2, 64, D), BF16)] * 5
-        + [rows(2), rows(2), rows(4), rows(4)]
-        + [tiles] * 4
+        + [rows(2), rows(2), rows(4), rows(4), rows(4)]
+        + [tiles] * 5
         + [vm((D, TOK), F32), vm((4, 80, D), F32), vm((4, 80, D), F32)]
         + halo
         + halo
@@ -566,11 +610,11 @@
         + [rows(2)] * 3
         + [vm((2, 2, TC, PAD_DIM, TOK), BF16)] * 2
         + [tiles] * 3
-        + [reduced(TC), reduced(TC), reduced(NX), reduced(NZ), reduced(TC)]
+        + [vm((3, 2, TC + 2, PAD_DIM, TOK), F32), reduced(2), reduced(NZ), reduced(HEADS)]
         + [vm((16, TOK), F32)] * 3
-        + [sem((5,)), sem((4, HEADS)), sem((4, 2)), sem((2, 2)), sem((2, 2))]
+        + [sem((5,)), sem((5, HEADS)), sem((5, 2)), sem((3, 2)), sem((3, 2))]
         + [sem((8,))] * 4
-        + [sem((2, 2, 4)), sem((2, 2)), sem((3, 2, TC)), sem((3,)), sem((4, 8)), sem((4,))],
+        + [sem((2, 2, 4)), sem((2, 2)), sem((3, 2, TC)), sem((3,)), sem((3, HEADS)), sem((3,))],
         compiler_params=pltpu.CompilerParams(collective_id=0, has_side_effects=True),
         name="whole",
     )(query, key, value, grad_out, control, kernel, detail_blocks)

time: 79.1 us -> 71.8 us (0.908); the launches traced: 78.9 us -> 70.8 us
  Pallas kernels: 78.3 us -> 70.1 us
    pallas_call x1, Pallas kernels: 76 us -> 67.9 us  [per_device(): pl.pallas_call(whole_kernel, out_shape=outs, in_specs=[pl.BlockSpec(memor...]
where the time goes in v4:
time: 71.8 us; the launch traced here: 70.8 us
  Pallas kernels  70.1 us (98%)
    pallas_call x1, Pallas kernels, per_device(): pl.pallas_call(whole_kernel, out_shape=outs, in_specs=[pl.BlockSpec(memor...  67.9 us
    pallas_call x1, Pallas kernels, per_device(): pl.pallas_call(copy_kernel, out_shape=outs, in_specs=vmem_specs(5), out_s...  2.27 us

profile of v4, /device:TPU:1, one launch (start us, length us, event | category | flops | bytes accessed | tf_op | source)
XLA Modules:
  0.0 70.8 jit_solution(7525768867812476911)
XLA Ops:
  0.6 67.9 %whole.1 = (bf16[2,64,1152]{2,1,0:T(8,128)(2,1)}, bf16[2,64,1152]{2,1,0:T(8,128)(2,1)}, bf16[2,64,1152]{2,1,0:T(8,128)(2,1)}, bf16[2,64,1152]{2,1,0:T(8,128)(2,1)}, f32[3,3,1152]{2,1,0:T(4,128)}) custom-call(bf16[2,64,1152]{2,1,0:T(8,128)(2,1)} %q_hbm.1, bf16[2,64,1152]{2,1,0:T(8,128)(2,1)} %k_hbm.1, bf16[2,64,1152]{2,1,0:T(8,128)(2,1)} %v_hbm.1, ...), custom_call_target="tpu_custom_call" | custom-call | tf_op jit(solution)/shard_map/whole/pallas_call | solution.py:595
  68.5 2.3 %finish.1 = (bf16[2,64,1152]{2,1,0:T(8,128)(2,1)}, bf16[2,64,1152]{2,1,0:T(8,128)(2,1)}, bf16[2,64,1152]{2,1,0:T(8,128)(2,1)}, bf16[2,64,1152]{2,1,0:T(8,128)(2,1)}, f32[3,3,1152]{2,1,0:T(4,128)}) custom-call(bf16[2,64,1152]{2,1,0:T(8,128)(2,1)} %get-tuple-element.10.refs_0_, bf16[2,64,1152]{2,1,0:T(8,128)(2,1)} %get-tuple-element.11.refs_1_, ...), custom_call_target="tpu_custom_call" | custom-call | tf_op jit(solution)/shard_map/finish/pallas_call | solution.py:621
